TPU v7x, 32 devices: a whole 2x2x4 slice. The times are simulated.
32 devices in a mesh: seq: 8 (over z, x), head: 4 (over y, core).
Axes of the slice: x: 2, y: 2, z: 4, core: 2. Of those that a mesh axis runs over, the one named last changes fastest.
Arguments:
- query_rows: bfloat16 [1, 2048, 2048], P(None, 'seq', 'head'), may hold values from -28 to 28
- key_rows: bfloat16 [1, 2048, 2048], P(None, 'seq', 'head'), may hold values from -4 to 4
- value_rows: bfloat16 [1, 2048, 2048], P(None, 'seq', 'head'), may hold values from -6 to 6
- grad_out: bfloat16 [1, 2048, 2048], P(None, 'seq', 'head'), may hold values from -6 to 6
- rand_blocks: int32 [1, 16, 32, 3], P(None, 'head'), may hold values from 0 to 31, as said below
- global_pos: int32 [128], replicated, may hold values from 0 to 2047, as said below
Outputs:
- attended: bfloat16 [1, 2048, 2048], P(None, 'seq', 'head')
- grad_query: bfloat16 [1, 2048, 2048], P(None, 'seq', 'head')
- grad_key: bfloat16 [1, 2048, 2048], P(None, 'seq', 'head')
- grad_value: bfloat16 [1, 2048, 2048], P(None, 'seq', 'head')
Inputs may be any that keep to these rules, and one draw needn't show every extreme that they name: `rand_blocks`: for each run of 4 query blocks and each run of 4 heads that start at multiples of these counts, taking the one sequence and all 3 picks together, at most 6 picks name a block of any one run of 4 key blocks that starts at a multiple of 4; in each such run of query blocks and heads some run of key blocks is named exactly 6 times. `global_pos`: distinct positions; the first and the last token of the sequence are among them.
All inputs are finite; a program needn't handle non-finite values.
Results may differ from a plain program's by a relative error of at most 0.006.
The roundings to bfloat16 on the way count: a program that leaves them out, or rounds other values in their place, can miss the bound.
Values may be sent and summed in bfloat16 or wider, within the bound.
No kernel may reach another device: no remote copies, remote signals or barrier semaphores. Data moves between devices by JAX's collectives and lax.ppermute only.
A program may use at most 64 MiB of HBM per device.

v0:
```python
import functools

import jax
import jax.numpy as jnp
from jax import lax
from jax.experimental import pallas as pl
from jax.experimental.pallas import tpu as pltpu
from jax.sharding import PartitionSpec as P


BLOCK = 64
AXES = ("seq", "head")
GROUPS = 2
CHUNK = 2
VMEM = pl.BlockSpec(memory_space=pltpu.VMEM)
SMEM = pl.BlockSpec(memory_space=pltpu.SMEM)
HBM = pl.BlockSpec(memory_space=pltpu.HBM)
F32 = jnp.float32
BF16 = jnp.bfloat16


def dot(a, b, dims):
    return lax.dot_general(a, b, (dims, ((), ())), preferred_element_type=F32)


def round_pairs(seq_count, head_count, i):
    rounds = seq_count // 2
    pairs = []
    for s in range(seq_count):
        for head in range(head_count):
            y, c = head // 2, head % 2
            k = rounds * c + (s + i) % rounds
            pairs.append((s * head_count + head, k * head_count + 2 * y + s // rounds))
    return pairs


def pack_kernel(rounds, width, pos_ref, a_ref, b_ref, *rest):
    outs, (buf, in_sem, out_sem) = rest[:rounds], rest[rounds:]
    s = pos_ref[0]
    loads = []
    for i in range(rounds):
        col = pl.multiple_of(lax.rem(s + i, rounds) * width, width)
        for n, ref in enumerate((a_ref, b_ref)):
            copy = pltpu.make_async_copy(
                ref.at[0, :, pl.ds(col, width)], buf.at[i, n], in_sem.at[i, n]
            )
            copy.start()
            loads.append(copy)
    stores = []
    for i in range(rounds):
        loads[2 * i].wait()
        loads[2 * i + 1].wait()
        copy = pltpu.make_async_copy(buf.at[i], outs[i], out_sem.at[i])
        copy.start()
        stores.append(copy)
    for copy in stores:
        copy.wait()


def pack(where, a, b, rounds):
    _, tokens, columns = a.shape
    width = columns // rounds
    out = jax.ShapeDtypeStruct((2, tokens, width), a.dtype)
    return pl.pallas_call(
        functools.partial(pack_kernel, rounds, width),
        out_shape=[out] * rounds,
        in_specs=[SMEM, HBM, HBM],
        out_specs=[HBM] * rounds,
        scratch_shapes=[
            pltpu.VMEM((rounds, 2, tokens, width), a.dtype),
            pltpu.SemaphoreType.DMA((rounds, 2)),
            pltpu.SemaphoreType.DMA((rounds,)),
        ],
        cost_estimate=pl.CostEstimate(
            flops=0, transcendentals=0, bytes_accessed=8 * tokens * columns
        ),
        name="pack",
    )(where, a, b)


def unpack_kernel(rounds, width, pos_ref, *rest):
    ins, outs, (buf, in_sem, out_sem) = rest[:rounds], rest[rounds : rounds + 2], rest[rounds + 2 :]
    s = pos_ref[0]
    loads = []
    for i in range(rounds):
        copy = pltpu.make_async_copy(ins[i], buf.at[i], in_sem.at[i])
        copy.start()
        loads.append(copy)
    stores = []
    for i in range(rounds):
        loads[i].wait()
        col = pl.multiple_of(lax.rem(s + i, rounds) * width, width)
        for n in range(2):
            copy = pltpu.make_async_copy(
                buf.at[i, n], outs[n].at[0, :, pl.ds(col, width)], out_sem.at[i, n]
            )
            copy.start()
            stores.append(copy)
    for copy in stores:
        copy.wait()


def unpack(where, parts):
    rounds = len(parts)
    _, tokens, width = parts[0].shape
    out = jax.ShapeDtypeStruct((1, tokens, rounds * width), parts[0].dtype)
    return pl.pallas_call(
        functools.partial(unpack_kernel, rounds, width),
        out_shape=[out] * 2,
        in_specs=[SMEM] + [HBM] * rounds,
        out_specs=[HBM] * 2,
        scratch_shapes=[
            pltpu.VMEM((rounds, 2, tokens, width), parts[0].dtype),
            pltpu.SemaphoreType.DMA((rounds,)),
            pltpu.SemaphoreType.DMA((rounds, 2)),
        ],
        cost_estimate=pl.CostEstimate(
            flops=0, transcendentals=0, bytes_accessed=8 * rounds * tokens * width
        ),
        name="unpack",
    )(where, *parts)


def slot_of(run, k, h, rounds):
    turn = (k - run % rounds) % rounds
    return jnp.where(run // rounds == h, 0, rounds) + turn


def first_rows(table, k, h, rounds, run_blocks):
    total, _ = table.shape
    runs = h * rounds + (k - jnp.arange(rounds)) % rounds
    blocks = (runs[:, None] * run_blocks + jnp.arange(run_blocks)[None, :]).reshape(-1)
    window = jnp.clip(blocks[:, None] + jnp.arange(-1, 2)[None, :], 0, total - 1)
    named = jnp.concatenate([window, table[blocks]], axis=1)
    place = slot_of(named // run_blocks, k, h, rounds) * run_blocks + named % run_blocks
    edge = (blocks == 0) + 2 * (blocks == total - 1)
    return (place * BLOCK).astype(jnp.int32).reshape(-1), edge.astype(jnp.int32)


def gather_kernel(rounds, rows_ref, *rest):
    parts, (all_ref, picked_ref, sem) = rest[: 2 * rounds], rest[2 * rounds :]
    tokens = all_ref.shape[1] // (2 * rounds)
    copies = []
    for n in range(2 * rounds):
        copy = pltpu.make_async_copy(
            parts[n], all_ref.at[:, pl.ds(n * tokens, tokens), :], sem.at[n]
        )
        copy.start()
        copies.append(copy)
    rows = rows_ref[...]
    count = rows.shape[0]
    sums = [None, None]
    for n in range(2 * rounds):
        ids = lax.broadcasted_iota(jnp.int32, (count, tokens), 1) + n * tokens
        hot = jnp.where(ids == rows, 1.0, 0.0).astype(BF16)
        copies[n].wait()
        for m in range(2):
            part = dot(hot, all_ref[m, n * tokens : (n + 1) * tokens], ((1,), (0,)))
            sums[m] = part if n == 0 else sums[m] + part
    for m in range(2):
        picked_ref[m] = sums[m].astype(BF16)


def gather(global_rows, own, other):
    rounds = len(own)
    _, tokens, width = own[0].shape
    count = global_rows.shape[0]
    return pl.pallas_call(
        functools.partial(gather_kernel, rounds),
        out_shape=[
            jax.ShapeDtypeStruct((2, 2 * rounds * tokens, width), BF16),
            jax.ShapeDtypeStruct((2, count, width), BF16),
        ],
        in_specs=[VMEM] + [HBM] * (2 * rounds),
        out_specs=[VMEM, VMEM],
        scratch_shapes=[pltpu.SemaphoreType.DMA((2 * rounds,))],
        cost_estimate=pl.CostEstimate(
            flops=8 * count * rounds * tokens * width,
            transcendentals=0,
            bytes_accessed=16 * rounds * tokens * width,
        ),
        name="gather",
    )(global_rows.reshape(count, 1), *own, *other)


def attend_kernel(run_blocks, listed, turns, rows_ref, edge_ref, all_ref, picked_ref, *rest):
    count = len(turns)
    sides, mixes, keeps = rest[:count], rest[count : 2 * count], rest[2 * count : 3 * count]
    side_buf, mix_buf, in_sem, out_sem = rest[3 * count :]
    loads, stores = [], []
    for n in range(count):
        copy = pltpu.make_async_copy(sides[n], side_buf.at[n], in_sem.at[n])
        copy.start()
        loads.append(copy)
    scale = all_ref.shape[2] ** -0.5
    column = lax.broadcasted_iota(jnp.int32, (1, 4 * BLOCK), 1)

    def begin(n, block):
        mine = slice(block * BLOCK, (block + 1) * BLOCK)
        query, grad = side_buf[n, 0, mine], side_buf[n, 1, mine]
        index = turns[n] * run_blocks + block
        rows = [
            pl.multiple_of(rows_ref[index * listed + m], BLOCK) for m in range(listed)
        ]
        keys, values = [
            jnp.concatenate(
                [all_ref[m, pl.ds(r, BLOCK)] for r in rows] + [picked_ref[m]], axis=0
            )
            for m in range(2)
        ]
        scores = dot(query, keys, ((1,), (1,))) * scale
        probs = dot(grad, values, ((1,), (1,)))
        edge = edge_ref[index]
        out = ((column < BLOCK) & (edge % 2 == 1)) | (
            (column >= 2 * BLOCK) & (column < 3 * BLOCK) & (edge >= 2)
        )
        near = jnp.where(out, -1e30, scores[:, : 4 * BLOCK])
        scores = jnp.concatenate([near, scores[:, 4 * BLOCK :]], axis=1)
        return n, mine, keys, values, scores, probs

    def finish(state):
        weighed = []
        for n, mine, keys, values, scores, probs in state:
            peak = jnp.max(scores, axis=1, keepdims=True)
            powers = jnp.exp(scores - peak)
            weights = powers * (1.0 / jnp.sum(powers, axis=1, keepdims=True))
            weights_b = weights.astype(BF16)
            keeps[n][1, mine] = weights_b
            weighed.append((weights, weights_b))
        scored = []
        for (n, mine, keys, values, scores, probs), (weights, weights_b) in zip(state, weighed):
            delta = jnp.sum(weights_b.astype(F32) * probs, axis=1, keepdims=True)
            dscore_b = (weights * (probs - delta)).astype(BF16)
            keeps[n][0, mine] = dscore_b
            scored.append(dscore_b)
        for (n, mine, keys, values, _, _), (_, weights_b), dscore_b in zip(
            state, weighed, scored
        ):
            mixed = dot(weights_b, values, ((1,), (0,)))
            grad_query = dot(dscore_b, keys, ((1,), (0,))) * scale
            mix_buf[n, 0, mine] = mixed.astype(BF16)
            mix_buf[n, 1, mine] = grad_query.astype(BF16)

    held = None
    for n in range(count):
        loads[n].wait()
        for block in range(0, run_blocks, CHUNK):
            state = [begin(n, b) for b in range(block, block + CHUNK)]
            if held is not None:
                finish(held)
                if block == 0:
                    copy = pltpu.make_async_copy(mix_buf.at[n - 1], mixes[n - 1], out_sem.at[n - 1])
                    copy.start()
                    stores.append(copy)
            held = state
    finish(held)
    copy = pltpu.make_async_copy(mix_buf.at[count - 1], mixes[count - 1], out_sem.at[count - 1])
    copy.start()
    stores.append(copy)
    for copy in stores:
        copy.wait()


def attend(rows, edge, all_kv, picked, sides, turns):
    _, tokens, width = sides[0].shape
    run_blocks = tokens // BLOCK
    listed = rows.shape[0] // edge.shape[0]
    entries = listed * BLOCK + picked.shape[1]
    count = len(turns)
    outs = pl.pallas_call(
        functools.partial(attend_kernel, run_blocks, listed, turns),
        out_shape=[jax.ShapeDtypeStruct((2, tokens, width), BF16)] * count
        + [jax.ShapeDtypeStruct((2, tokens, entries), BF16)] * count,
        in_specs=[SMEM, SMEM, VMEM, VMEM] + [HBM] * count,
        out_specs=[HBM] * count + [VMEM] * count,
        scratch_shapes=[
            pltpu.VMEM((count, 2, tokens, width), BF16),
            pltpu.VMEM((count, 2, tokens, width), BF16),
            pltpu.SemaphoreType.DMA((count,)),
            pltpu.SemaphoreType.DMA((count,)),
        ],
        cost_estimate=pl.CostEstimate(
            flops=8 * count * tokens * entries * width,
            transcendentals=count * tokens * entries,
            bytes_accessed=4 * all_kv.size,
        ),
        name="attend",
    )(rows, edge, all_kv, picked, *sides)
    return outs[:count], outs[count:]


def key_grads_kernel(rounds, run_blocks, listed, rows_ref, *rest):
    sides, keeps = rest[:rounds], rest[rounds : 2 * rounds]
    acc, other_ref, side_buf, in_sem, out_sem = rest[2 * rounds :]
    loads = []
    for turn in range(rounds):
        copy = pltpu.make_async_copy(sides[turn], side_buf.at[turn], in_sem.at[turn])
        copy.start()
        loads.append(copy)
    entries = listed * BLOCK
    half = rounds * run_blocks * BLOCK
    acc[:, : 2 * half] = jnp.zeros((2, 2 * half, acc.shape[2]), F32)
    for copy in loads:
        copy.wait()
    for n in range(2):
        shared = None
        for turn in range(rounds):
            part = dot(keeps[turn][n, :, entries:], side_buf[turn, n], ((0,), (0,)))
            shared = part if shared is None else shared + part
        acc[n, 2 * half :] = shared
    for turn in range(rounds):
        for block in range(run_blocks):
            index = turn * run_blocks + block
            mine = slice(block * BLOCK, (block + 1) * BLOCK)
            parts = [
                dot(keeps[turn][n, mine, :entries], side_buf[turn, n, mine], ((0,), (0,)))
                for n in range(2)
            ]
            for m in range(listed):
                row = pl.multiple_of(rows_ref[index * listed + m], BLOCK)
                for n in range(2):
                    acc[n, pl.ds(row, BLOCK)] += parts[n][m * BLOCK : (m + 1) * BLOCK]
    stores = [
        pltpu.make_async_copy(
            acc.at[:, pl.ds(half, acc.shape[1] - half), :], other_ref, out_sem.at[0]
        )
    ]
    for copy in stores:
        copy.start()
    for copy in stores:
        copy.wait()


def key_grads(rows, sides, keeps):
    rounds = len(sides)
    _, tokens, width = sides[0].shape
    run_blocks = tokens // BLOCK
    listed = rows.shape[0] // (rounds * run_blocks)
    entries = keeps[0].shape[2]
    half, count = rounds * tokens, entries - listed * BLOCK
    return pl.pallas_call(
        functools.partial(key_grads_kernel, rounds, run_blocks, listed),
        out_shape=[
            jax.ShapeDtypeStruct((2, 2 * half + count, width), F32),
            jax.ShapeDtypeStruct((2, half + count, width), F32),
        ],
        in_specs=[SMEM] + [HBM] * rounds + [VMEM] * rounds,
        out_specs=[VMEM, HBM],
        scratch_shapes=[
            pltpu.VMEM((rounds, 2, tokens, width), BF16),
            pltpu.SemaphoreType.DMA((rounds,)),
            pltpu.SemaphoreType.DMA((1,)),
        ],
        cost_estimate=pl.CostEstimate(
            flops=4 * rounds * tokens * entries * width,
            transcendentals=0,
            bytes_accessed=4 * rounds * tokens * (entries + 4 * width),
        ),
        name="key_grads",
    )(rows, *sides, *keeps)


def total_kernel(rounds, rows_ref, acc_ref, came_ref, *rest):
    outs, (came_buf, out_buf, in_sem, out_sem) = rest[:rounds], rest[rounds:]
    load = pltpu.make_async_copy(came_ref, came_buf, in_sem.at[0])
    load.start()
    tokens, width = outs[0].shape[1:]
    half = rounds * tokens
    count = rows_ref.shape[1]
    scale = width**-0.5
    rows = rows_ref[...]
    load.wait()
    halves = []
    for n in range(2):
        shared = acc_ref[n, 2 * half :] + came_buf[n, half:]
        high = shared.astype(BF16)
        halves += [high, (shared - high.astype(F32)).astype(BF16)]
    halves = jnp.concatenate(halves, axis=1)
    stores = []
    for i in range(rounds):
        ids = lax.broadcasted_iota(jnp.int32, (tokens, count), 0) + i * tokens
        hot = jnp.where(ids == rows, 1.0, 0.0).astype(BF16)
        spread = dot(hot, halves, ((1,), (0,)))
        mine = slice(i * tokens, (i + 1) * tokens)
        for n in range(2):
            whole = acc_ref[n, mine] + came_buf[n, mine]
            whole = whole + spread[:, 2 * n * width : (2 * n + 1) * width]
            whole = whole + spread[:, (2 * n + 1) * width : (2 * n + 2) * width]
            if n == 0:
                whole = whole * scale
            out_buf[i, n] = whole.astype(BF16)
        copy = pltpu.make_async_copy(out_buf.at[i], outs[i], out_sem.at[i])
        copy.start()
        stores.append(copy)
    for copy in stores:
        copy.wait()


def total(global_rows, acc, came, rounds):
    rows, width = came.shape[1:]
    count = global_rows.shape[0]
    tokens = (rows - count) // rounds
    return pl.pallas_call(
        functools.partial(total_kernel, rounds),
        out_shape=[jax.ShapeDtypeStruct((2, tokens, width), BF16)] * rounds,
        in_specs=[VMEM, VMEM, HBM],
        out_specs=[HBM] * rounds,
        scratch_shapes=[
            pltpu.VMEM(came.shape, F32),
            pltpu.VMEM((rounds, 2, tokens, width), BF16),
            pltpu.SemaphoreType.DMA((1,)),
            pltpu.SemaphoreType.DMA((rounds,)),
        ],
        cost_estimate=pl.CostEstimate(
            flops=4 * rows * width, transcendentals=0, bytes_accessed=20 * rows * width
        ),
        name="total",
    )(global_rows.reshape(1, count), acc, came)


def by_heads(query_rows, key_rows, value_rows, grad_out, rand_blocks, global_pos):
    seq_count, head_count = lax.axis_size("seq"), lax.axis_size("head")
    _, rounds, _, _ = rand_blocks.shape
    tokens = query_rows.shape[1]
    run_blocks = tokens // BLOCK
    k, head_index = lax.axis_index("seq"), lax.axis_index("head")
    h = head_index % 2
    where = k.astype(jnp.int32).reshape(1)
    sibling = [(i, i ^ 1) for i in range(head_count)]
    there = [round_pairs(seq_count, head_count, i) for i in range(rounds)]
    back = [[(j, i) for i, j in pairs] for pairs in there]

    def send(parts, pairs):
        out = []
        for n, part in enumerate(parts):
            out.append(lax.ppermute(part, AXES, pairs[n]))
        return out

    def swap(parts):
        out = []
        for part in parts:
            out.append(lax.ppermute(part, "head", sibling))
        return out

    kv = send(pack(where, key_rows, value_rows, rounds), there)
    sides = send(pack(where, query_rows, grad_out, rounds), there)
    (other_table,) = swap([rand_blocks])
    kv_other = swap(kv)
    tables = jnp.where(k // rounds == h, rand_blocks, other_table)
    table = lax.dynamic_index_in_dim(tables[0], k % rounds, 0, keepdims=False)
    rows, edge = first_rows(table, k, h, rounds, run_blocks)
    global_rows = slot_of(global_pos // tokens, k, h, rounds) * tokens + global_pos % tokens
    global_rows = global_rows.astype(jnp.int32)

    all_kv, picked = gather(global_rows, kv, kv_other)
    mixes, keeps = [], []
    for n in range(GROUPS):
        turns = tuple(range(n * rounds // GROUPS, (n + 1) * rounds // GROUPS))
        mix, keep = attend(rows, edge, all_kv, picked, [sides[t] for t in turns], turns)
        mixes += mix
        keeps += keep
    mixes = send(mixes, back)
    acc, other = key_grads(rows, sides, keeps)
    (came,) = swap([other])
    grads = total(global_rows, acc, came, rounds)
    grads = send(grads, back)
    attended, grad_query = unpack(where, mixes)
    grad_key, grad_value = unpack(where, grads)
    return attended, grad_query, grad_key, grad_value


def extended_2(value, sides, width):
    for axis, dim in sides:
        size, length = (lax.axis_size(axis), value.shape[dim])
        up = [(i, (i + 1) % size) for i in range(size - 1)]
        down = [(j, i) for i, j in up]
        last = lax.slice_in_dim(value, length - width, length, axis=dim)
        first = lax.slice_in_dim(value, 0, width, axis=dim)
        before = lax.ppermute(last, axis, up)
        after = lax.ppermute(first, axis, down)
        value = jnp.concatenate([before, value, after], axis=dim)
    return value


def by_blocks(query_rows, key_rows, value_rows, grad_out, rand_blocks, global_pos):
    batch_count, tok_local, columns = query_rows.shape
    seq_count = lax.axis_size("seq")
    seq_index = lax.axis_index("seq")
    heads_local = rand_blocks.shape[1]
    total_blocks = rand_blocks.shape[2]
    pick_count = rand_blocks.shape[3]
    head_dim = columns // heads_local
    blocks_local = tok_local // BLOCK
    score_scale = head_dim ** (-0.5)
    slot_count = batch_count * heads_local * blocks_local * pick_count
    capacity = (slot_count + seq_count - 1) // seq_count
    buffer_rows = seq_count * capacity
    f32 = jnp.float32
    bf16 = jnp.bfloat16

    def to_blocks(array):
        return array.reshape(batch_count, blocks_local, BLOCK, heads_local, head_dim).transpose(
            0, 3, 1, 2, 4
        )

    def from_blocks(array):
        return array.transpose(0, 2, 3, 1, 4).reshape(batch_count, tok_local, columns)

    def pair_blocks(array):
        return array.reshape(2, batch_count, blocks_local, BLOCK, heads_local, head_dim).transpose(
            0, 1, 4, 2, 3, 5
        )

    def global_sum(array):
        return lax.psum(array, "seq")

    key_value = jnp.stack([key_rows, value_rows])
    edge_rows = jnp.concatenate([key_value[:, :, :BLOCK], key_value[:, :, -BLOCK:]], axis=2)
    extended = extended_2(edge_rows, (("seq", 2),), BLOCK)
    padded = jnp.concatenate([extended[:, :, :BLOCK], key_value, extended[:, :, -BLOCK:]], axis=2)

    def shifted(start):
        return pair_blocks(padded[:, :, start : start + tok_local])

    window_lists = jnp.concatenate([shifted(0), shifted(BLOCK), shifted(2 * BLOCK)], axis=4)
    my_table = lax.dynamic_slice_in_dim(
        rand_blocks, seq_index * blocks_local, blocks_local, 2
    ).reshape(slot_count)
    holder = my_table // blocks_local
    holder_hot = (holder[:, None] == jnp.arange(seq_count)[None, :]).astype(jnp.int32)
    holder_rank = jnp.sum((jnp.cumsum(holder_hot, axis=0) - 1) * holder_hot, axis=1)
    position = holder * capacity + holder_rank
    requests = rand_blocks.reshape(batch_count, heads_local, seq_count, blocks_local, pick_count)
    requests = requests.transpose(2, 0, 1, 3, 4).reshape(seq_count, slot_count)
    wanted = (requests // blocks_local == seq_index).astype(jnp.int32)
    wanted_rank = jnp.cumsum(wanted, axis=1) - 1
    chosen = wanted[:, None, :] * (
        wanted_rank[:, None, :] == jnp.arange(capacity)[None, :, None]
    ).astype(jnp.int32)
    slot_live = (jnp.sum(chosen, axis=2) > 0).reshape(buffer_rows)
    slot_index = jnp.sum(chosen * jnp.arange(slot_count)[None, None, :], axis=2)
    which_batch = slot_index // (heads_local * blocks_local * pick_count)
    which_head = slot_index // (blocks_local * pick_count) % heads_local
    which_block = jnp.take_along_axis(requests, slot_index, axis=1) % blocks_local
    stacked = key_value.reshape(
        2, batch_count, blocks_local, BLOCK, heads_local, head_dim
    ).transpose(1, 2, 4, 0, 3, 5)
    outgoing = stacked[which_batch, which_block, which_head].reshape(
        buffer_rows, 2, BLOCK, head_dim
    )
    incoming = lax.all_to_all(outgoing, "seq", split_axis=0, concat_axis=0, tiled=True)
    fetched = incoming[position].reshape(
        batch_count, heads_local, blocks_local, pick_count, 2, BLOCK, head_dim
    )
    fetched = fetched.transpose(4, 0, 1, 2, 3, 5, 6).reshape(
        2, batch_count, heads_local, blocks_local, pick_count * BLOCK, head_dim
    )
    local_pos = global_pos - seq_index * tok_local
    pick_hot = (local_pos[:, None] == jnp.arange(tok_local)[None, :]).astype(bf16)
    owned_rows = jnp.einsum("gt,pbtc->pbgc", pick_hot, key_value, preferred_element_type=f32)
    shared = global_sum(owned_rows).astype(bf16)
    globals_count = shared.shape[2]
    global_kv = shared.reshape(2, batch_count, globals_count, heads_local, head_dim).transpose(
        0, 1, 3, 2, 4
    )
    global_kv = jnp.broadcast_to(
        global_kv[:, :, :, None],
        (2, batch_count, heads_local, blocks_local, globals_count, head_dim),
    )
    lists_all = jnp.concatenate([window_lists, fetched, global_kv], axis=4)
    key_lists = lists_all[0]
    value_lists = lists_all[1]
    key_count = key_lists.shape[3]
    block_ids = seq_index * blocks_local + jnp.arange(blocks_local)
    column_ids = jnp.arange(key_count)[None, :]
    middle_ok = jnp.where(
        (column_ids >= 2 * BLOCK) & (column_ids < 3 * BLOCK),
        (block_ids < total_blocks - 1)[:, None],
        True,
    )
    valid_mask = jnp.where(column_ids < BLOCK, (block_ids > 0)[:, None], middle_ok)
    query_blocks = to_blocks(query_rows)
    grad_blocks = to_blocks(grad_out)
    scores = (
        jnp.einsum("bhjqd,bhjkd->bhjqk", query_blocks, key_lists, preferred_element_type=f32)
        * score_scale
    )
    scores = jnp.where(valid_mask[None, None, :, None, :], scores, -1e30)
    row_max = jnp.max(scores, axis=-1, keepdims=True)
    log_total = row_max + jnp.log(jnp.sum(jnp.exp(scores - row_max), axis=-1, keepdims=True))
    weights = jnp.exp(scores - log_total)
    weights_b = weights.astype(bf16)
    mixed_rows = jnp.einsum(
        "bhjqk,bhjkd->bhjqd", weights_b, value_lists, preferred_element_type=f32
    )
    attended = from_blocks(mixed_rows.astype(bf16))
    row_delta = jnp.sum(grad_blocks.astype(f32) * mixed_rows, axis=-1, keepdims=True)
    grad_probs = jnp.einsum(
        "bhjqd,bhjkd->bhjqk", grad_blocks, value_lists, preferred_element_type=f32
    )
    dscore_b = (weights * (grad_probs - row_delta)).astype(bf16)
    grad_query = (
        jnp.einsum("bhjqk,bhjkd->bhjqd", dscore_b, key_lists, preferred_element_type=f32)
        * score_scale
    )

    def key_grads(lower, upper):
        key_part = (
            jnp.einsum(
                "bhjqk,bhjqd->bhjkd",
                dscore_b[..., lower:upper],
                query_blocks,
                preferred_element_type=f32,
            )
            * score_scale
        )
        value_part = jnp.einsum(
            "bhjqk,bhjqd->bhjkd",
            weights_b[..., lower:upper],
            grad_blocks,
            preferred_element_type=f32,
        )
        return jnp.stack([key_part, value_part])

    window_cols = 3 * BLOCK
    random_cols = pick_count * BLOCK
    window_grads = key_grads(0, window_cols).reshape(
        2, batch_count, heads_local, blocks_local, 3, BLOCK, head_dim
    )
    padded_grads = jnp.pad(
        window_grads[:, :, :, :, 0], ((0, 0), (0, 0), (0, 0), (0, 2), (0, 0), (0, 0))
    )
    padded_grads = padded_grads + jnp.pad(
        window_grads[:, :, :, :, 1], ((0, 0), (0, 0), (0, 0), (1, 1), (0, 0), (0, 0))
    )
    padded_grads = padded_grads + jnp.pad(
        window_grads[:, :, :, :, 2], ((0, 0), (0, 0), (0, 0), (2, 0), (0, 0), (0, 0))
    )
    own_grads = padded_grads[:, :, :, 1:-1]
    rim_grads = jnp.stack([padded_grads[:, :, :, 0], padded_grads[:, :, :, -1]], axis=3)
    returned = extended_2(rim_grads.astype(jnp.bfloat16), (("seq", 3),), 1).astype(rim_grads.dtype)
    own_grads = own_grads.at[:, :, :, 0].add(returned[:, :, :, 0])
    own_grads = own_grads.at[:, :, :, -1].add(returned[:, :, :, 3])
    global_grads = jnp.sum(key_grads(window_cols + random_cols, key_count), axis=3)
    global_grads = global_grads.transpose(0, 1, 3, 2, 4).reshape(
        2, batch_count, globals_count, columns
    )
    global_summed = global_sum(global_grads)
    inside = (local_pos >= 0) & (local_pos < tok_local)
    safe_pos = jnp.where(inside, local_pos, tok_local)
    global_local = (
        jnp.zeros((2, batch_count, tok_local, columns), f32)
        .at[:, :, safe_pos]
        .add(global_summed, mode="drop")
    )
    global_part = pair_blocks(global_local)
    target = ((which_batch * blocks_local + which_block) * heads_local + which_head).reshape(
        buffer_rows
    )
    random_grads = key_grads(window_cols, window_cols + random_cols)
    per_slot = random_grads.reshape(
        2, batch_count, heads_local, blocks_local, pick_count, BLOCK, head_dim
    )
    per_slot = per_slot.transpose(1, 2, 3, 4, 0, 5, 6).reshape(slot_count, 2, BLOCK, head_dim)
    sending = jnp.zeros((buffer_rows, 2, BLOCK, head_dim), f32).at[position].set(per_slot)
    arrived = lax.all_to_all(
        sending.astype(jnp.bfloat16), "seq", split_axis=0, concat_axis=0, tiled=True
    ).astype(sending.dtype)
    kept = jnp.where(slot_live[:, None, None, None], arrived, 0.0)
    summed = (
        jnp.zeros((batch_count * blocks_local * heads_local, 2, BLOCK, head_dim), f32)
        .at[target]
        .add(kept)
    )
    random_part = summed.reshape(
        batch_count, blocks_local, heads_local, 2, BLOCK, head_dim
    ).transpose(3, 0, 2, 1, 4, 5)
    total_grads = own_grads + random_part + global_part
    grad_key = from_blocks(total_grads[0].astype(bf16))
    grad_value = from_blocks(total_grads[1].astype(bf16))
    return (attended, from_blocks(grad_query.astype(bf16)), grad_key, grad_value)


def body(query_rows, key_rows, value_rows, grad_out, rand_blocks, global_pos):
    seq_count, head_count = lax.axis_size("seq"), lax.axis_size("head")
    batch_count, heads_local = rand_blocks.shape[:2]
    whole_heads = seq_count == 2 * heads_local and head_count % 2 == 0 and batch_count == 1
    form = by_heads if whole_heads else by_blocks
    return form(query_rows, key_rows, value_rows, grad_out, rand_blocks, global_pos)


def solution(mesh):
    return jax.shard_map(
        body,
        mesh=mesh,
        in_specs=(
            P(None, "seq", "head"),
            P(None, "seq", "head"),
            P(None, "seq", "head"),
            P(None, "seq", "head"),
            P(None, "head", None, None),
            P(),
        ),
        out_specs=(
            P(None, "seq", "head"),
            P(None, "seq", "head"),
            P(None, "seq", "head"),
            P(None, "seq", "head"),
        ),
        check_vma=False,
    )
```

profile of v0, /device:TPU:3, one launch (start us, length us, event | category | flops | bytes accessed | tf_op | source)
XLA Modules:
  0.0 93.2 jit_solution(13134961553583459729)
XLA Ops:
  0.6 0.7 collective-permute-start
  1.4 1.8 %pack.3 = (bf16[2,256,128]{2,1,0:T(8,128)(2,1)}, bf16[2,256,128]{2,1,0:T(8,128)(2,1)}, bf16[2,256,128]{2,1,0:T(8,128)(2,1)}, bf16[2,256,128]{2,1,0:T(8,128)(2,1)}) custom-call(s32[1]{0:T(128)} %bitcast.pos_ref, bf16[1,256,512]{2,1,0:T(8,128)(2,1)} %a_ref.3, bf16[1,256,512]{2,1,0:T(8,128)(2,1)} %b_ref.3), custom_call_target="tpu_custom_call" | custom-call | bytes 1048576 | tf_op jit(solution)/shard_map/pack/pallas_call | solution.py:64
  3.2 4.1 %collective-permute-start.9 = (bf16[2,256,128]{2,1,0:T(8,128)(2,1)}, bf16[2,256,128]{2,1,0:T(8,128)(2,1)S(1)}, u32[]{:S(2)}, u32[]{:S(2)}) collective-permute-start(bf16[2,256,128]{2,1,0:T(8,128)(2,1)} %get-tuple-element.38), channel_id=1, source_target_pairs={{0,0},{1,16},{2,2},{3,18},{4,4},{5,20},{6,6},{7,22},{8,8},{9,24},{... | collective-permute-start | bytes 393224 | tf_op jit(solution)/shard_map/ppermute | solution.py:436
  7.3 1.8 %pack.2 = (bf16[2,256,128]{2,1,0:T(8,128)(2,1)}, bf16[2,256,128]{2,1,0:T(8,128)(2,1)}, bf16[2,256,128]{2,1,0:T(8,128)(2,1)}, bf16[2,256,128]{2,1,0:T(8,128)(2,1)}) custom-call(s32[1]{0:T(128)} %bitcast.pos_ref, bf16[1,256,512]{2,1,0:T(8,128)(2,1)} %a_ref.2, bf16[1,256,512]{2,1,0:T(8,128)(2,1)} %b_ref.2), custom_call_target="tpu_custom_call" | custom-call | bytes 1048576 | tf_op jit(solution)/shard_map/pack/pallas_call | solution.py:64
  9.2 2.3 %collective-permute-start.1 = (bf16[2,256,128]{2,1,0:T(8,128)(2,1)}, bf16[2,256,128]{2,1,0:T(8,128)(2,1)S(1)}, u32[]{:S(2)}, u32[]{:S(2)}) collective-permute-start(bf16[2,256,128]{2,1,0:T(8,128)(2,1)} %get-tuple-element.32), channel_id=1, source_target_pairs={{0,0},{1,16},{2,2},{3,18},{4,4},{5,20},{6,6},{7,22},{8,8},{9,24},{... | collective-permute-start | bytes 393224 | tf_op jit(solution)/shard_map/ppermute | solution.py:436
  11.5 3.3 %collective-permute-start.2 = (bf16[2,256,128]{2,1,0:T(8,128)(2,1)}, bf16[2,256,128]{2,1,0:T(8,128)(2,1)S(1)}, u32[]{:S(2)}, u32[]{:S(2)}) collective-permute-start(bf16[2,256,128]{2,1,0:T(8,128)(2,1)} %get-tuple-element.33), channel_id=1, source_target_pairs={{0,4},{1,20},{2,6},{3,22},{4,8},{5,24},{6,10},{7,26},{8,12},{9,28}... | collective-permute-start | bytes 393224 | tf_op jit(solution)/shard_map/ppermute | solution.py:436
  14.8 0.1 collective-permute-start.3
  14.9 0.1 iota_add_fusion
  15.0 0.1 add.153
  15.1 0.1 add.160
  15.2 0.7 fusion.15
  15.8 0.5 fusion.7.edge_ref
  16.4 0.1 add_clamp_fusion
  16.5 0.7 copy.13.rows_ref
  17.2 0.0 collective-permute-done
  17.2 2.6 %collective-permute-start.4 = (bf16[2,256,128]{2,1,0:T(8,128)(2,1)}, bf16[2,256,128]{2,1,0:T(8,128)(2,1)S(1)}, u32[]{:S(2)}, u32[]{:S(2)}) collective-permute-start(bf16[2,256,128]{2,1,0:T(8,128)(2,1)} %get-tuple-element.35), channel_id=1, source_target_pairs={{0,12},{1,28},{2,14},{3,30},{4,0},{5,16},{6,2},{7,18},{8,4},{9,20}... | collective-permute-start | bytes 393224 | tf_op jit(solution)/shard_map/ppermute | solution.py:436
  19.8 0.0 collective-permute-start.5
  19.8 2.4 %collective-permute-done.2.rest_1_ = bf16[2,256,128]{2,1,0:T(8,128)(2,1)S(1)} collective-permute-done((bf16[2,256,128]{2,1,0:T(8,128)(2,1)}, bf16[2,256,128]{2,1,0:T(8,128)(2,1)S(1)}, u32[]{:S(2)}, u32[]{:S(2)}) %collective-permute-start.2) | collective-permute-done | bytes 131104 | tf_op jit(solution)/shard_map/ppermute | solution.py:436
  22.2 0.0 collective-permute-done.3.rest_2_
  22.2 0.0 copy-start.7
  22.2 0.5 collective-permute-start.7
  22.7 0.7 broadcast_select_fusion
  23.4 0.1 copy.14
  23.5 0.6 gather_fusion
  24.1 0.1 pad_add_fusion
  24.1 0.1 concatenate.6
  24.2 0.4 collective-permute-done.4.rest_3_
  24.6 4.1 %collective-permute-start.10 = (bf16[2,256,128]{2,1,0:T(8,128)(2,1)}, bf16[2,256,128]{2,1,0:T(8,128)(2,1)S(1)}, u32[]{:S(2)}, u32[]{:S(2)}) collective-permute-start(bf16[2,256,128]{2,1,0:T(8,128)(2,1)} %get-tuple-element.39), channel_id=1, source_target_pairs={{0,4},{1,20},{2,6},{3,22},{4,8},{5,24},{6,10},{7,26},{8,12},{9,28}... | collective-permute-start | bytes 393224 | tf_op jit(solution)/shard_map/ppermute | solution.py:436
  28.7 2.2 %collective-permute-start.13 = (bf16[2,256,128]{2,1,0:T(8,128)(2,1)}, bf16[2,256,128]{2,1,0:T(8,128)(2,1)S(1)}, u32[]{:S(2)}, u32[]{:S(2)}) collective-permute-start(bf16[2,256,128]{2,1,0:T(8,128)(2,1)} %get-tuple-element.42), channel_id=1, source_target_pairs={{0,8},{1,24},{2,10},{3,26},{4,12},{5,28},{6,14},{7,30},{8,0},{9,16... | collective-permute-start | bytes 393224 | tf_op jit(solution)/shard_map/ppermute | solution.py:436
  30.9 0.1 collective-permute-start.8
  31.0 0.6 fusion.13.rows_ref
  31.6 0.8 collective-permute-done.8.rest_7_
  32.4 0.6 copy-done.20
  33.0 4.0 %gather.7 = (bf16[2,2048,128]{2,1,0:T(8,128)(2,1)}, bf16[2,128,128]{2,1,0:T(8,128)(2,1)}) custom-call(s32[128,1]{1,0:T(8,128)} %copy.13.rows_ref, bf16[2,256,128]{2,1,0:T(8,128)(2,1)} %copy-done.5, bf16[2,256,128]{2,1,0:T(8,128)(2,1)} %copy-done.6, bf16[2,256,128]{2,1,0:T(8,128)(2,1)} %copy-done.7, bf16[2,256,128]{2,1,0:T(8,128)(2,1)} %copy-done.8, ...), custom_call_target="tpu_custom_call" | custom-call | flops 134217728 | bytes 2097152 | tf_op jit(solution)/shard_map/gather/pallas_call | solution.py:168
  37.0 1.2 %collective-permute-done.14.rest_1_.rest_3_ = bf16[2,256,128]{2,1,0:T(8,128)(2,1)S(1)} collective-permute-done((bf16[2,256,128]{2,1,0:T(8,128)(2,1)}, bf16[2,256,128]{2,1,0:T(8,128)(2,1)S(1)}, u32[]{:S(2)}, u32[]{:S(2)}) %collective-permute-start.14) | collective-permute-done | bytes 131104 | tf_op jit(solution)/shard_map/ppermute | solution.py:436
  38.2 0.7 copy-done.4
  38.8 5.7 %attend.3 = (bf16[2,256,128]{2,1,0:T(8,128)(2,1)}, bf16[2,256,128]{2,1,0:T(8,128)(2,1)}, bf16[2,256,512]{2,1,0:T(8,128)(2,1)}, bf16[2,256,512]{2,1,0:T(8,128)(2,1)}) custom-call(s32[96]{0:T(128)} %fusion.13.rows_ref, s32[16]{0:T(128)} %fusion.7.edge_ref, bf16[2,2048,128]{2,1,0:T(8,128)(2,1)} %get-tuple-element.36.all_ref, ...), custom_call_target="tpu_custom_call" | custom-call | flops 268435456 | bytes 2097152 | tf_op jit(solution)/shard_map/attend/pallas_call | solution.py:270
  44.5 0.0 copy-start.1
  44.6 0.6 copy-done.1
  45.2 0.7 copy-done.2
  45.8 5.7 %attend.2 = (bf16[2,256,128]{2,1,0:T(8,128)(2,1)}, bf16[2,256,128]{2,1,0:T(8,128)(2,1)}, bf16[2,256,512]{2,1,0:T(8,128)(2,1)}, bf16[2,256,512]{2,1,0:T(8,128)(2,1)}) custom-call(s32[96]{0:T(128)} %fusion.13.rows_ref, s32[16]{0:T(128)} %fusion.7.edge_ref, bf16[2,2048,128]{2,1,0:T(8,128)(2,1)} %get-tuple-element.36.all_ref, ...), custom_call_target="tpu_custom_call" | custom-call | flops 268435456 | bytes 2097152 | tf_op jit(solution)/shard_map/attend/pallas_call | solution.py:270
  51.6 0.0 copy-start.24
  51.6 0.0 copy-start.21
  51.6 0.0 copy-start.22
  51.6 6.4 %key_grads.1 = (f32[2,2176,128]{2,1,0:T(8,128)}, f32[2,1152,128]{2,1,0:T(8,128)}) custom-call(s32[96]{0:T(128)} %fusion.13.rows_ref, bf16[2,256,128]{2,1,0:T(8,128)(2,1)} %copy-done.1, bf16[2,256,128]{2,1,0:T(8,128)(2,1)} %copy-done.2, bf16[2,256,128]{2,1,0:T(8,128)(2,1)} %copy-done.3, bf16[2,256,128]{2,1,0:T(8,128)(2,1)} %copy-done.4, ...), custom_call_target="tpu_custom_call" | custom-call | flops 268435456 | bytes 4194304 | tf_op jit(solution)/shard_map/key_grads/pallas_call | solution.py:341
  58.0 0.1 collective-permute-start.17
  58.1 2.1 %collective-permute-start.15 = (bf16[2,256,128]{2,1,0:T(8,128)(2,1)S(1)}, bf16[2,256,128]{2,1,0:T(8,128)(2,1)S(1)}, u32[]{:S(2)}, u32[]{:S(2)}) collective-permute-start(bf16[2,256,128]{2,1,0:T(8,128)(2,1)S(1)} %copy-done.25), channel_id=1, source_target_pairs={{8,0},{24,1},{10,2},{26,3},{12,4},{28,5},{14,6},{30,7},{0,8},{16,9... | collective-permute-start | bytes 393224 | tf_op jit(solution)/shard_map/ppermute | solution.py:436
  60.2 2.7 %collective-permute-start.16 = (bf16[2,256,128]{2,1,0:T(8,128)(2,1)S(1)}, bf16[2,256,128]{2,1,0:T(8,128)(2,1)S(1)}, u32[]{:S(2)}, u32[]{:S(2)}) collective-permute-start(bf16[2,256,128]{2,1,0:T(8,128)(2,1)S(1)} %copy-done.23), channel_id=1, source_target_pairs={{12,0},{28,1},{14,2},{30,3},{0,4},{16,5},{2,6},{18,7},{4,8},{20,9}... | collective-permute-start | bytes 393224 | tf_op jit(solution)/shard_map/ppermute | solution.py:436
  62.9 1.9 %collective-permute-start.11 = (bf16[2,256,128]{2,1,0:T(8,128)(2,1)S(1)}, bf16[2,256,128]{2,1,0:T(8,128)(2,1)S(1)}, u32[]{:S(2)}, u32[]{:S(2)}) collective-permute-start(bf16[2,256,128]{2,1,0:T(8,128)(2,1)S(1)} %copy-done.24), channel_id=1, source_target_pairs={{0,0},{16,1},{2,2},{18,3},{4,4},{20,5},{6,6},{22,7},{8,8},{24,9},{... | collective-permute-start | bytes 393224 | tf_op jit(solution)/shard_map/ppermute | solution.py:436
  64.8 0.5 fusion.14.rows_ref
  65.3 1.4 %collective-permute-start.12 = (bf16[2,256,128]{2,1,0:T(8,128)(2,1)S(1)}, bf16[2,256,128]{2,1,0:T(8,128)(2,1)S(1)}, u32[]{:S(2)}, u32[]{:S(2)}) collective-permute-start(bf16[2,256,128]{2,1,0:T(8,128)(2,1)S(1)} %copy-done.22), channel_id=1, source_target_pairs={{4,0},{20,1},{6,2},{22,3},{8,4},{24,5},{10,6},{26,7},{12,8},{28,9}... | collective-permute-start | bytes 393224 | tf_op jit(solution)/shard_map/ppermute | solution.py:436
  66.7 1.0 %copy-done = f32[2,1152,128]{2,1,0:T(8,128)} copy-done((f32[2,1152,128]{2,1,0:T(8,128)}, f32[2,1152,128]{2,1,0:T(8,128)S(1)}, u32[]{:S(2)}) %copy-start) | copy-done | bytes 1179672
  67.7 4.0 %total.1 = (bf16[2,256,128]{2,1,0:T(8,128)(2,1)}, bf16[2,256,128]{2,1,0:T(8,128)(2,1)}, bf16[2,256,128]{2,1,0:T(8,128)(2,1)}, bf16[2,256,128]{2,1,0:T(8,128)(2,1)}) custom-call(s32[1,128]{1,0:T(1,128)} %fusion.14.rows_ref, f32[2,2176,128]{2,1,0:T(8,128)} %get-tuple-element.52.acc_ref, f32[2,1152,128]{2,1,0:T(8,128)} %copy-done), custom_call_target="tpu_custom_call" | custom-call | flops 589824 | bytes 2949120 | tf_op jit(solution)/shard_map/total/pallas_call | solution.py:403
  71.8 4.1 %collective-permute-start.18 = (bf16[2,256,128]{2,1,0:T(8,128)(2,1)}, bf16[2,256,128]{2,1,0:T(8,128)(2,1)S(1)}, u32[]{:S(2)}, u32[]{:S(2)}) collective-permute-start(bf16[2,256,128]{2,1,0:T(8,128)(2,1)} %get-tuple-element.54), channel_id=1, source_target_pairs={{0,0},{16,1},{2,2},{18,3},{4,4},{20,5},{6,6},{22,7},{8,8},{24,9},{... | collective-permute-start | bytes 393224 | tf_op jit(solution)/shard_map/ppermute | solution.py:436
  75.9 2.2 %collective-permute-start.19 = (bf16[2,256,128]{2,1,0:T(8,128)(2,1)}, bf16[2,256,128]{2,1,0:T(8,128)(2,1)S(1)}, u32[]{:S(2)}, u32[]{:S(2)}) collective-permute-start(bf16[2,256,128]{2,1,0:T(8,128)(2,1)} %get-tuple-element.55), channel_id=1, source_target_pairs={{4,0},{20,1},{6,2},{22,3},{8,4},{24,5},{10,6},{26,7},{12,8},{28,9}... | collective-permute-start | bytes 393224 | tf_op jit(solution)/shard_map/ppermute | solution.py:436
  78.1 1.4 %collective-permute-start.20 = (bf16[2,256,128]{2,1,0:T(8,128)(2,1)}, bf16[2,256,128]{2,1,0:T(8,128)(2,1)S(1)}, u32[]{:S(2)}, u32[]{:S(2)}) collective-permute-start(bf16[2,256,128]{2,1,0:T(8,128)(2,1)} %get-tuple-element.56), channel_id=1, source_target_pairs={{8,0},{24,1},{10,2},{26,3},{12,4},{28,5},{14,6},{30,7},{0,8},{16,9... | collective-permute-start | bytes 393224 | tf_op jit(solution)/shard_map/ppermute | solution.py:436
  79.5 2.4 %collective-permute-start.21 = (bf16[2,256,128]{2,1,0:T(8,128)(2,1)}, bf16[2,256,128]{2,1,0:T(8,128)(2,1)S(1)}, u32[]{:S(2)}, u32[]{:S(2)}) collective-permute-start(bf16[2,256,128]{2,1,0:T(8,128)(2,1)} %get-tuple-element.57), channel_id=1, source_target_pairs={{12,0},{28,1},{14,2},{30,3},{0,4},{16,5},{2,6},{18,7},{4,8},{20,9}... | collective-permute-start | bytes 393224 | tf_op jit(solution)/shard_map/ppermute | solution.py:436
  81.9 0.0 copy-start.16
  81.9 0.6 copy-done.16
  82.6 1.8 %unpack.2 = (bf16[1,256,512]{2,1,0:T(8,128)(2,1)}, bf16[1,256,512]{2,1,0:T(8,128)(2,1)}) custom-call(s32[1]{0:T(128)} %bitcast.pos_ref, bf16[2,256,128]{2,1,0:T(8,128)(2,1)} %copy-done.14, bf16[2,256,128]{2,1,0:T(8,128)(2,1)} %copy-done.16, bf16[2,256,128]{2,1,0:T(8,128)(2,1)} %copy-done.11, bf16[2,256,128]{2,1,0:T(8,128)(2,1)} %copy-done.12), custom_call_target="tpu_custom_call" | custom-call | bytes 1048576 | tf_op jit(solution)/shard_map/unpack/pallas_call | solution.py:107
  84.5 0.1 collective-permute-done.20.rest_2_
  84.6 6.1 %collective-permute-done.21.rest_3_ = bf16[2,256,128]{2,1,0:T(8,128)(2,1)S(1)} collective-permute-done((bf16[2,256,128]{2,1,0:T(8,128)(2,1)}, bf16[2,256,128]{2,1,0:T(8,128)(2,1)S(1)}, u32[]{:S(2)}, u32[]{:S(2)}) %collective-permute-start.21) | collective-permute-done | bytes 131104 | tf_op jit(solution)/shard_map/ppermute | solution.py:436
  90.7 0.6 copy-done.19
  91.4 1.8 %unpack.3 = (bf16[1,256,512]{2,1,0:T(8,128)(2,1)}, bf16[1,256,512]{2,1,0:T(8,128)(2,1)}) custom-call(s32[1]{0:T(128)} %bitcast.pos_ref, bf16[2,256,128]{2,1,0:T(8,128)(2,1)} %copy-done.15, bf16[2,256,128]{2,1,0:T(8,128)(2,1)} %copy-done.17, bf16[2,256,128]{2,1,0:T(8,128)(2,1)} %copy-done.18, bf16[2,256,128]{2,1,0:T(8,128)(2,1)} %copy-done.19), custom_call_target="tpu_custom_call" | custom-call | bytes 1048576 | tf_op jit(solution)/shard_map/unpack/pallas_call | solution.py:107
  (59 shorter events, 0.1 us)
Async XLA Ops:
  0.6 16.6 %collective-permute-start = (s32[1,4,32,3]{2,1,3,0:T(4,128)}, s32[1,4,32,3]{2,1,3,0:T(4,128)S(1)}, u32[]{:S(2)}, u32[]{:S(2)}) collective-permute-start(s32[1,4,32,3]{2,1,3,0:T(4,128)} %param.10), channel_id=1, source_target_pairs={{0,1},{1,0},{2,3},{3,2},{4,5},{5,4},{6,7},{7,6},{8,9},{9,8},{10,11... | collective-permute-start | bytes 4616 | tf_op jit(solution)/shard_map/ppermute | solution.py:442
  3.2 41.3 %collective-permute-start.9 = (bf16[2,256,128]{2,1,0:T(8,128)(2,1)}, bf16[2,256,128]{2,1,0:T(8,128)(2,1)S(1)}, u32[]{:S(2)}, u32[]{:S(2)}) collective-permute-start(bf16[2,256,128]{2,1,0:T(8,128)(2,1)} %get-tuple-element.38), channel_id=1, source_target_pairs={{0,0},{1,16},{2,2},{3,18},{4,4},{5,20},{6,6},{7,22},{8,8},{9,24},{... | collective-permute-start | bytes 393224 | tf_op jit(solution)/shard_map/ppermute | solution.py:436
  9.2 10.6 %collective-permute-start.1 = (bf16[2,256,128]{2,1,0:T(8,128)(2,1)}, bf16[2,256,128]{2,1,0:T(8,128)(2,1)S(1)}, u32[]{:S(2)}, u32[]{:S(2)}) collective-permute-start(bf16[2,256,128]{2,1,0:T(8,128)(2,1)} %get-tuple-element.32), channel_id=1, source_target_pairs={{0,0},{1,16},{2,2},{3,18},{4,4},{5,20},{6,6},{7,22},{8,8},{9,24},{... | collective-permute-start | bytes 393224 | tf_op jit(solution)/shard_map/ppermute | solution.py:436
  11.5 10.7 %collective-permute-start.2 = (bf16[2,256,128]{2,1,0:T(8,128)(2,1)}, bf16[2,256,128]{2,1,0:T(8,128)(2,1)S(1)}, u32[]{:S(2)}, u32[]{:S(2)}) collective-permute-start(bf16[2,256,128]{2,1,0:T(8,128)(2,1)} %get-tuple-element.33), channel_id=1, source_target_pairs={{0,4},{1,20},{2,6},{3,22},{4,8},{5,24},{6,10},{7,26},{8,12},{9,28}... | collective-permute-start | bytes 393224 | tf_op jit(solution)/shard_map/ppermute | solution.py:436
  14.8 7.4 %collective-permute-start.3 = (bf16[2,256,128]{2,1,0:T(8,128)(2,1)}, bf16[2,256,128]{2,1,0:T(8,128)(2,1)S(1)}, u32[]{:S(2)}, u32[]{:S(2)}) collective-permute-start(bf16[2,256,128]{2,1,0:T(8,128)(2,1)} %get-tuple-element.34), channel_id=1, source_target_pairs={{0,8},{1,24},{2,10},{3,26},{4,12},{5,28},{6,14},{7,30},{8,0},{9,16... | collective-permute-start | bytes 393224 | tf_op jit(solution)/shard_map/ppermute | solution.py:436
  17.2 7.4 %collective-permute-start.4 = (bf16[2,256,128]{2,1,0:T(8,128)(2,1)}, bf16[2,256,128]{2,1,0:T(8,128)(2,1)S(1)}, u32[]{:S(2)}, u32[]{:S(2)}) collective-permute-start(bf16[2,256,128]{2,1,0:T(8,128)(2,1)} %get-tuple-element.35), channel_id=1, source_target_pairs={{0,12},{1,28},{2,14},{3,30},{4,0},{5,16},{6,2},{7,18},{8,4},{9,20}... | collective-permute-start | bytes 393224 | tf_op jit(solution)/shard_map/ppermute | solution.py:436
  19.8 12.5 %copy-start.5 = (bf16[2,256,128]{2,1,0:T(8,128)(2,1)}, bf16[2,256,128]{2,1,0:T(8,128)(2,1)S(1)}, u32[]{:S(2)}) copy-start(bf16[2,256,128]{2,1,0:T(8,128)(2,1)S(1)} %collective-permute-done.1.rest_0_) | copy-start | bytes 393220
  19.8 8.9 %collective-permute-start.5 = (bf16[2,256,128]{2,1,0:T(8,128)(2,1)S(1)}, bf16[2,256,128]{2,1,0:T(8,128)(2,1)S(1)}, u32[]{:S(2)}, u32[]{:S(2)}) collective-permute-start(bf16[2,256,128]{2,1,0:T(8,128)(2,1)S(1)} %collective-permute-done.1.rest_0_), channel_id=1, source_target_pairs={{0,1},{1,0},{2,3},{3,2},{4,5},{5,4},{6,7},{7,6},{8,9},{9,8},{10,11... | collective-permute-start | bytes 393224 | tf_op jit(solution)/shard_map/ppermute | solution.py:442
  22.2 10.1 %copy-start.6 = (bf16[2,256,128]{2,1,0:T(8,128)(2,1)}, bf16[2,256,128]{2,1,0:T(8,128)(2,1)S(1)}, u32[]{:S(2)}) copy-start(bf16[2,256,128]{2,1,0:T(8,128)(2,1)S(1)} %collective-permute-done.2.rest_1_) | copy-start | bytes 393220
  22.2 8.7 %collective-permute-start.6 = (bf16[2,256,128]{2,1,0:T(8,128)(2,1)S(1)}, bf16[2,256,128]{2,1,0:T(8,128)(2,1)S(1)}, u32[]{:S(2)}, u32[]{:S(2)}) collective-permute-start(bf16[2,256,128]{2,1,0:T(8,128)(2,1)S(1)} %collective-permute-done.2.rest_1_), channel_id=1, source_target_pairs={{0,1},{1,0},{2,3},{3,2},{4,5},{5,4},{6,7},{7,6},{8,9},{9,8},{10,11... | collective-permute-start | bytes 393224 | tf_op jit(solution)/shard_map/ppermute | solution.py:442
  22.2 10.1 %copy-start.7 = (bf16[2,256,128]{2,1,0:T(8,128)(2,1)}, bf16[2,256,128]{2,1,0:T(8,128)(2,1)S(1)}, u32[]{:S(2)}) copy-start(bf16[2,256,128]{2,1,0:T(8,128)(2,1)S(1)} %collective-permute-done.3.rest_2_) | copy-start | bytes 393220
  22.2 8.7 %collective-permute-start.7 = (bf16[2,256,128]{2,1,0:T(8,128)(2,1)S(1)}, bf16[2,256,128]{2,1,0:T(8,128)(2,1)S(1)}, u32[]{:S(2)}, u32[]{:S(2)}) collective-permute-start(bf16[2,256,128]{2,1,0:T(8,128)(2,1)S(1)} %collective-permute-done.3.rest_2_), channel_id=1, source_target_pairs={{0,1},{1,0},{2,3},{3,2},{4,5},{5,4},{6,7},{7,6},{8,9},{9,8},{10,11... | collective-permute-start | bytes 393224 | tf_op jit(solution)/shard_map/ppermute | solution.py:442
  24.6 7.7 %copy-start.8 = (bf16[2,256,128]{2,1,0:T(8,128)(2,1)}, bf16[2,256,128]{2,1,0:T(8,128)(2,1)S(1)}, u32[]{:S(2)}) copy-start(bf16[2,256,128]{2,1,0:T(8,128)(2,1)S(1)} %collective-permute-done.4.rest_3_) | copy-start | bytes 393220
  24.6 19.9 %collective-permute-start.10 = (bf16[2,256,128]{2,1,0:T(8,128)(2,1)}, bf16[2,256,128]{2,1,0:T(8,128)(2,1)S(1)}, u32[]{:S(2)}, u32[]{:S(2)}) collective-permute-start(bf16[2,256,128]{2,1,0:T(8,128)(2,1)} %get-tuple-element.39), channel_id=1, source_target_pairs={{0,4},{1,20},{2,6},{3,22},{4,8},{5,24},{6,10},{7,26},{8,12},{9,28}... | collective-permute-start | bytes 393224 | tf_op jit(solution)/shard_map/ppermute | solution.py:436
  28.7 3.6 %copy-start.9 = (bf16[2,256,128]{2,1,0:T(8,128)(2,1)}, bf16[2,256,128]{2,1,0:T(8,128)(2,1)S(1)}, u32[]{:S(2)}) copy-start(bf16[2,256,128]{2,1,0:T(8,128)(2,1)S(1)} %collective-permute-done.5.rest_4_) | copy-start | bytes 393220
  28.7 8.3 %collective-permute-start.13 = (bf16[2,256,128]{2,1,0:T(8,128)(2,1)}, bf16[2,256,128]{2,1,0:T(8,128)(2,1)S(1)}, u32[]{:S(2)}, u32[]{:S(2)}) collective-permute-start(bf16[2,256,128]{2,1,0:T(8,128)(2,1)} %get-tuple-element.42), channel_id=1, source_target_pairs={{0,8},{1,24},{2,10},{3,26},{4,12},{5,28},{6,14},{7,30},{8,0},{9,16... | collective-permute-start | bytes 393224 | tf_op jit(solution)/shard_map/ppermute | solution.py:436
  30.9 1.5 %copy-start.10 = (bf16[2,256,128]{2,1,0:T(8,128)(2,1)}, bf16[2,256,128]{2,1,0:T(8,128)(2,1)S(1)}, u32[]{:S(2)}) copy-start(bf16[2,256,128]{2,1,0:T(8,128)(2,1)S(1)} %collective-permute-done.6.rest_5_) | copy-start | bytes 393220
  30.9 7.3 %collective-permute-start.14 = (bf16[2,256,128]{2,1,0:T(8,128)(2,1)}, bf16[2,256,128]{2,1,0:T(8,128)(2,1)S(1)}, u32[]{:S(2)}, u32[]{:S(2)}) collective-permute-start(bf16[2,256,128]{2,1,0:T(8,128)(2,1)} %get-tuple-element.43), channel_id=1, source_target_pairs={{0,12},{1,28},{2,14},{3,30},{4,0},{5,16},{6,2},{7,18},{8,4},{9,20}... | collective-permute-start | bytes 393224 | tf_op jit(solution)/shard_map/ppermute | solution.py:436
  30.9 1.5 %copy-start.13 = (bf16[2,256,128]{2,1,0:T(8,128)(2,1)}, bf16[2,256,128]{2,1,0:T(8,128)(2,1)S(1)}, u32[]{:S(2)}) copy-start(bf16[2,256,128]{2,1,0:T(8,128)(2,1)S(1)} %collective-permute-done.7.rest_6_) | copy-start | bytes 393220
  30.9 1.4 %collective-permute-start.8 = (bf16[2,256,128]{2,1,0:T(8,128)(2,1)S(1)}, bf16[2,256,128]{2,1,0:T(8,128)(2,1)S(1)}, u32[]{:S(2)}, u32[]{:S(2)}) collective-permute-start(bf16[2,256,128]{2,1,0:T(8,128)(2,1)S(1)} %collective-permute-done.4.rest_3_), channel_id=1, source_target_pairs={{0,1},{1,0},{2,3},{3,2},{4,5},{5,4},{6,7},{7,6},{8,9},{9,8},{10,11... | collective-permute-start | bytes 393224 | tf_op jit(solution)/shard_map/ppermute | solution.py:442
  32.4 0.6 copy-start.20
  37.0 1.2 %copy-start.3 = (bf16[2,256,128]{2,1,0:T(8,128)(2,1)}, bf16[2,256,128]{2,1,0:T(8,128)(2,1)S(1)}, u32[]{:S(2)}) copy-start(bf16[2,256,128]{2,1,0:T(8,128)(2,1)S(1)} %collective-permute-done.13.rest_0_.rest_2_) | copy-start | bytes 393220
  38.2 0.7 copy-start.4
  44.5 0.7 copy-start.1
  45.2 0.7 copy-start.2
  51.6 6.5 %copy-start.25 = (bf16[2,256,128]{2,1,0:T(8,128)(2,1)S(1)}, bf16[2,256,128]{2,1,0:T(8,128)(2,1)}, u32[]{:S(2)}) copy-start(bf16[2,256,128]{2,1,0:T(8,128)(2,1)} %get-tuple-element.44) | copy-start | bytes 393220
  51.6 8.6 %copy-start.23 = (bf16[2,256,128]{2,1,0:T(8,128)(2,1)S(1)}, bf16[2,256,128]{2,1,0:T(8,128)(2,1)}, u32[]{:S(2)}) copy-start(bf16[2,256,128]{2,1,0:T(8,128)(2,1)} %get-tuple-element.45) | copy-start | bytes 393220
  51.6 11.3 %copy-start.24 = (bf16[2,256,128]{2,1,0:T(8,128)(2,1)S(1)}, bf16[2,256,128]{2,1,0:T(8,128)(2,1)}, u32[]{:S(2)}) copy-start(bf16[2,256,128]{2,1,0:T(8,128)(2,1)} %get-tuple-element.40) | copy-start | bytes 393220
  51.6 13.2 %copy-start.21 = (s32[128]{0:T(128)S(1)}, s32[128]{0:T(128)}, u32[]{:S(2)}) copy-start(s32[128]{0:T(128)} %param.11) | copy-start | bytes 1540
  51.6 13.7 %copy-start.22 = (bf16[2,256,128]{2,1,0:T(8,128)(2,1)S(1)}, bf16[2,256,128]{2,1,0:T(8,128)(2,1)}, u32[]{:S(2)}) copy-start(bf16[2,256,128]{2,1,0:T(8,128)(2,1)} %get-tuple-element.41) | copy-start | bytes 393220
  58.0 8.7 %collective-permute-start.17 = (f32[2,1152,128]{2,1,0:T(8,128)}, f32[2,1152,128]{2,1,0:T(8,128)S(1)}, u32[]{:S(2)}, u32[]{:S(2)}) collective-permute-start(f32[2,1152,128]{2,1,0:T(8,128)} %get-tuple-element.53), channel_id=1, source_target_pairs={{0,1},{1,0},{2,3},{3,2},{4,5},{5,4},{6,7},{7,6},{8,9},{9,8},{10,11... | collective-permute-start | bytes 3538952 | tf_op jit(solution)/shard_map/ppermute | solution.py:442
  58.1 17.7 %collective-permute-start.15 = (bf16[2,256,128]{2,1,0:T(8,128)(2,1)S(1)}, bf16[2,256,128]{2,1,0:T(8,128)(2,1)S(1)}, u32[]{:S(2)}, u32[]{:S(2)}) collective-permute-start(bf16[2,256,128]{2,1,0:T(8,128)(2,1)S(1)} %copy-done.25), channel_id=1, source_target_pairs={{8,0},{24,1},{10,2},{26,3},{12,4},{28,5},{14,6},{30,7},{0,8},{16,9... | collective-permute-start | bytes 393224 | tf_op jit(solution)/shard_map/ppermute | solution.py:436
  60.2 17.9 %collective-permute-start.16 = (bf16[2,256,128]{2,1,0:T(8,128)(2,1)S(1)}, bf16[2,256,128]{2,1,0:T(8,128)(2,1)S(1)}, u32[]{:S(2)}, u32[]{:S(2)}) collective-permute-start(bf16[2,256,128]{2,1,0:T(8,128)(2,1)S(1)} %copy-done.23), channel_id=1, source_target_pairs={{12,0},{28,1},{14,2},{30,3},{0,4},{16,5},{2,6},{18,7},{4,8},{20,9}... | collective-permute-start | bytes 393224 | tf_op jit(solution)/shard_map/ppermute | solution.py:436
  62.9 16.6 %collective-permute-start.11 = (bf16[2,256,128]{2,1,0:T(8,128)(2,1)S(1)}, bf16[2,256,128]{2,1,0:T(8,128)(2,1)S(1)}, u32[]{:S(2)}, u32[]{:S(2)}) collective-permute-start(bf16[2,256,128]{2,1,0:T(8,128)(2,1)S(1)} %copy-done.24), channel_id=1, source_target_pairs={{0,0},{16,1},{2,2},{18,3},{4,4},{20,5},{6,6},{22,7},{8,8},{24,9},{... | collective-permute-start | bytes 393224 | tf_op jit(solution)/shard_map/ppermute | solution.py:436
  65.3 16.6 %collective-permute-start.12 = (bf16[2,256,128]{2,1,0:T(8,128)(2,1)S(1)}, bf16[2,256,128]{2,1,0:T(8,128)(2,1)S(1)}, u32[]{:S(2)}, u32[]{:S(2)}) collective-permute-start(bf16[2,256,128]{2,1,0:T(8,128)(2,1)S(1)} %copy-done.22), channel_id=1, source_target_pairs={{4,0},{20,1},{6,2},{22,3},{8,4},{24,5},{10,6},{26,7},{12,8},{28,9}... | collective-permute-start | bytes 393224 | tf_op jit(solution)/shard_map/ppermute | solution.py:436
  66.7 1.0 %copy-start = (f32[2,1152,128]{2,1,0:T(8,128)}, f32[2,1152,128]{2,1,0:T(8,128)S(1)}, u32[]{:S(2)}) copy-start(f32[2,1152,128]{2,1,0:T(8,128)S(1)} %collective-permute-done.17.came_ref) | copy-start | bytes 3538948
  71.8 12.7 %collective-permute-start.18 = (bf16[2,256,128]{2,1,0:T(8,128)(2,1)}, bf16[2,256,128]{2,1,0:T(8,128)(2,1)S(1)}, u32[]{:S(2)}, u32[]{:S(2)}) collective-permute-start(bf16[2,256,128]{2,1,0:T(8,128)(2,1)} %get-tuple-element.54), channel_id=1, source_target_pairs={{0,0},{16,1},{2,2},{18,3},{4,4},{20,5},{6,6},{22,7},{8,8},{24,9},{... | collective-permute-start | bytes 393224 | tf_op jit(solution)/shard_map/ppermute | solution.py:436
  75.8 6.1 %copy-start.11 = (bf16[2,256,128]{2,1,0:T(8,128)(2,1)}, bf16[2,256,128]{2,1,0:T(8,128)(2,1)S(1)}, u32[]{:S(2)}) copy-start(bf16[2,256,128]{2,1,0:T(8,128)(2,1)S(1)} %collective-permute-done.15.rest_2_) | copy-start | bytes 393220
  75.9 8.6 %collective-permute-start.19 = (bf16[2,256,128]{2,1,0:T(8,128)(2,1)}, bf16[2,256,128]{2,1,0:T(8,128)(2,1)S(1)}, u32[]{:S(2)}, u32[]{:S(2)}) collective-permute-start(bf16[2,256,128]{2,1,0:T(8,128)(2,1)} %get-tuple-element.55), channel_id=1, source_target_pairs={{4,0},{20,1},{6,2},{22,3},{8,4},{24,5},{10,6},{26,7},{12,8},{28,9}... | collective-permute-start | bytes 393224 | tf_op jit(solution)/shard_map/ppermute | solution.py:436
  78.1 3.8 %copy-start.12 = (bf16[2,256,128]{2,1,0:T(8,128)(2,1)}, bf16[2,256,128]{2,1,0:T(8,128)(2,1)S(1)}, u32[]{:S(2)}) copy-start(bf16[2,256,128]{2,1,0:T(8,128)(2,1)S(1)} %collective-permute-done.16.rest_3_) | copy-start | bytes 393220
  78.1 6.5 %collective-permute-start.20 = (bf16[2,256,128]{2,1,0:T(8,128)(2,1)}, bf16[2,256,128]{2,1,0:T(8,128)(2,1)S(1)}, u32[]{:S(2)}, u32[]{:S(2)}) collective-permute-start(bf16[2,256,128]{2,1,0:T(8,128)(2,1)} %get-tuple-element.56), channel_id=1, source_target_pairs={{8,0},{24,1},{10,2},{26,3},{12,4},{28,5},{14,6},{30,7},{0,8},{16,9... | collective-permute-start | bytes 393224 | tf_op jit(solution)/shard_map/ppermute | solution.py:436
  79.5 2.4 %copy-start.14 = (bf16[2,256,128]{2,1,0:T(8,128)(2,1)}, bf16[2,256,128]{2,1,0:T(8,128)(2,1)S(1)}, u32[]{:S(2)}) copy-start(bf16[2,256,128]{2,1,0:T(8,128)(2,1)S(1)} %collective-permute-done.11.rest_0_) | copy-start | bytes 393220
  79.5 11.2 %collective-permute-start.21 = (bf16[2,256,128]{2,1,0:T(8,128)(2,1)}, bf16[2,256,128]{2,1,0:T(8,128)(2,1)S(1)}, u32[]{:S(2)}, u32[]{:S(2)}) collective-permute-start(bf16[2,256,128]{2,1,0:T(8,128)(2,1)} %get-tuple-element.57), channel_id=1, source_target_pairs={{12,0},{28,1},{14,2},{30,3},{0,4},{16,5},{2,6},{18,7},{4,8},{20,9}... | collective-permute-start | bytes 393224 | tf_op jit(solution)/shard_map/ppermute | solution.py:436
  81.9 0.7 copy-start.16
  84.4 6.3 %copy-start.15 = (bf16[2,256,128]{2,1,0:T(8,128)(2,1)}, bf16[2,256,128]{2,1,0:T(8,128)(2,1)S(1)}, u32[]{:S(2)}) copy-start(bf16[2,256,128]{2,1,0:T(8,128)(2,1)S(1)} %collective-permute-done.18.rest_0_) | copy-start | bytes 393220
  84.5 6.2 %copy-start.17 = (bf16[2,256,128]{2,1,0:T(8,128)(2,1)}, bf16[2,256,128]{2,1,0:T(8,128)(2,1)S(1)}, u32[]{:S(2)}) copy-start(bf16[2,256,128]{2,1,0:T(8,128)(2,1)S(1)} %collective-permute-done.19.rest_1_) | copy-start | bytes 393220
  84.6 6.1 %copy-start.18 = (bf16[2,256,128]{2,1,0:T(8,128)(2,1)}, bf16[2,256,128]{2,1,0:T(8,128)(2,1)S(1)}, u32[]{:S(2)}) copy-start(bf16[2,256,128]{2,1,0:T(8,128)(2,1)S(1)} %collective-permute-done.20.rest_2_) | copy-start | bytes 393220
  90.7 0.7 copy-start.19
where the time goes:
time: 93.9 us; the launch traced here: 93.2 us
  starting transfers between devices  38.1 us (41%)
  Pallas kernels  33.2 us (35%)
  waiting for transfers between devices  11 us (12%)
  local copies, waits for them, and re-layouts  6.64 us (7%)
  other arithmetic  3.26 us (3%)
  between operations  1.06 us (1%)
    ppermute x16, starting transfers between devices, send(): out.append(lax.ppermute(part, AXES, pairs[n]))  36.7 us
    pallas_call x2, Pallas kernels, attend(): pl.pallas_call(functools.partial(attend_kernel, run_blocks, listed, turns...  11.4 us
    ppermute x16, waiting for transfers between devices, send(): out.append(lax.ppermute(part, AXES, pairs[n]))  10.2 us
    pallas_call x1, Pallas kernels, key_grads(): pl.pallas_call(functools.partial(key_grads_kernel, rounds, run_blocks, li...  6.4 us
    unnamed x52, local copies, waits for them, and re-layouts  4.99 us
    pallas_call x1, Pallas kernels, total(): pl.pallas_call(functools.partial(total_kernel, rounds), out_shape=[jax.Sh...  4.03 us
    pallas_call x1, Pallas kernels, gather(): pl.pallas_call(functools.partial(gather_kernel, rounds), out_shape=[jax.S...  3.99 us
    pallas_call x2, Pallas kernels, unpack(): pl.pallas_call(functools.partial(unpack_kernel, rounds, width), out_shape...  3.69 us
  transfers between devices with their start and end apart: 22, of which 6 were waited for; matrix products, arithmetic and copies ran while one was open for 5% of the time, Pallas kernels for 21%

commit v1 on v0

--- a/solution.py
+++ b/solution.py
@@ -12,8 +12,10 @@
 AXES = ("seq", "head")
 GROUPS = 2
 CHUNK = 2
+GRANT = 24 * 1024 * 1024
 VMEM = pl.BlockSpec(memory_space=pltpu.VMEM)
 SMEM = pl.BlockSpec(memory_space=pltpu.SMEM)
+PARAMS = pltpu.CompilerParams(vmem_limit_bytes=GRANT)
 HBM = pl.BlockSpec(memory_space=pltpu.HBM)
 F32 = jnp.float32
 BF16 = jnp.bfloat16
@@ -29,7 +31,7 @@
     for s in range(seq_count):
         for head in range(head_count):
             y, c = head // 2, head % 2
-            k = rounds * c + (s + i) % rounds
+            k = rounds * c + (s % rounds ^ i)
             pairs.append((s * head_count + head, k * head_count + 2 * y + s // rounds))
     return pairs
 
@@ -39,7 +41,7 @@
     s = pos_ref[0]
     loads = []
     for i in range(rounds):
-        col = pl.multiple_of(lax.rem(s + i, rounds) * width, width)
+        col = pl.multiple_of((lax.rem(s, rounds) ^ i) * width, width)
         for n, ref in enumerate((a_ref, b_ref)):
             copy = pltpu.make_async_copy(
                 ref.at[0, :, pl.ds(col, width)], buf.at[i, n], in_sem.at[i, n]
@@ -71,6 +73,7 @@
             pltpu.SemaphoreType.DMA((rounds, 2)),
             pltpu.SemaphoreType.DMA((rounds,)),
         ],
+        compiler_params=PARAMS,
         cost_estimate=pl.CostEstimate(
             flops=0, transcendentals=0, bytes_accessed=8 * tokens * columns
         ),
@@ -89,7 +92,7 @@
     stores = []
     for i in range(rounds):
         loads[i].wait()
-        col = pl.multiple_of(lax.rem(s + i, rounds) * width, width)
+        col = pl.multiple_of((lax.rem(s, rounds) ^ i) * width, width)
         for n in range(2):
             copy = pltpu.make_async_copy(
                 buf.at[i, n], outs[n].at[0, :, pl.ds(col, width)], out_sem.at[i, n]
@@ -114,6 +117,7 @@
             pltpu.SemaphoreType.DMA((rounds,)),
             pltpu.SemaphoreType.DMA((rounds, 2)),
         ],
+        compiler_params=PARAMS,
         cost_estimate=pl.CostEstimate(
             flops=0, transcendentals=0, bytes_accessed=8 * rounds * tokens * width
         ),
@@ -122,13 +126,13 @@
 
 
 def slot_of(run, k, h, rounds):
-    turn = (k - run % rounds) % rounds
+    turn = (k ^ run) % rounds
     return jnp.where(run // rounds == h, 0, rounds) + turn
 
 
 def first_rows(table, k, h, rounds, run_blocks):
     total, _ = table.shape
-    runs = h * rounds + (k - jnp.arange(rounds)) % rounds
+    runs = h * rounds + (k % rounds ^ jnp.arange(rounds))
     blocks = (runs[:, None] * run_blocks + jnp.arange(run_blocks)[None, :]).reshape(-1)
     window = jnp.clip(blocks[:, None] + jnp.arange(-1, 2)[None, :], 0, total - 1)
     named = jnp.concatenate([window, table[blocks]], axis=1)
@@ -174,6 +178,7 @@
         in_specs=[VMEM] + [HBM] * (2 * rounds),
         out_specs=[VMEM, VMEM],
         scratch_shapes=[pltpu.SemaphoreType.DMA((2 * rounds,))],
+        compiler_params=PARAMS,
         cost_estimate=pl.CostEstimate(
             flops=8 * count * rounds * tokens * width,
             transcendentals=0,
@@ -279,6 +284,7 @@
             pltpu.SemaphoreType.DMA((count,)),
             pltpu.SemaphoreType.DMA((count,)),
         ],
+        compiler_params=PARAMS,
         cost_estimate=pl.CostEstimate(
             flops=8 * count * tokens * entries * width,
             transcendentals=count * tokens * entries,
@@ -351,6 +357,7 @@
             pltpu.SemaphoreType.DMA((rounds,)),
             pltpu.SemaphoreType.DMA((1,)),
         ],
+        compiler_params=PARAMS,
         cost_estimate=pl.CostEstimate(
             flops=4 * rounds * tokens * entries * width,
             transcendentals=0,
@@ -411,6 +418,7 @@
             pltpu.SemaphoreType.DMA((1,)),
             pltpu.SemaphoreType.DMA((rounds,)),
         ],
+        compiler_params=PARAMS,
         cost_estimate=pl.CostEstimate(
             flops=4 * rows * width, transcendentals=0, bytes_accessed=20 * rows * width
         ),
@@ -428,7 +436,6 @@
     where = k.astype(jnp.int32).reshape(1)
     sibling = [(i, i ^ 1) for i in range(head_count)]
     there = [round_pairs(seq_count, head_count, i) for i in range(rounds)]
-    back = [[(j, i) for i, j in pairs] for pairs in there]
 
     def send(parts, pairs):
         out = []
@@ -459,11 +466,11 @@
         mix, keep = attend(rows, edge, all_kv, picked, [sides[t] for t in turns], turns)
         mixes += mix
         keeps += keep
-    mixes = send(mixes, back)
+    mixes = send(mixes, there)
     acc, other = key_grads(rows, sides, keeps)
     (came,) = swap([other])
     grads = total(global_rows, acc, came, rounds)
-    grads = send(grads, back)
+    grads = send(grads, there)
     attended, grad_query = unpack(where, mixes)
     grad_key, grad_value = unpack(where, grads)
     return attended, grad_query, grad_key, grad_value
@@ -684,7 +691,8 @@
 def body(query_rows, key_rows, value_rows, grad_out, rand_blocks, global_pos):
     seq_count, head_count = lax.axis_size("seq"), lax.axis_size("head")
     batch_count, heads_local = rand_blocks.shape[:2]
-    whole_heads = seq_count == 2 * heads_local and head_count % 2 == 0 and batch_count == 1
+    whole_heads = seq_count == 2 * heads_local and heads_local & (heads_local - 1) == 0
+    whole_heads = whole_heads and head_count % 2 == 0 and batch_count == 1
     form = by_heads if whole_heads else by_blocks
     return form(query_rows, key_rows, value_rows, grad_out, rand_blocks, global_pos)
 

time: 93.9 us -> 78.4 us (0.83)
  the two profiles are of different devices: /device:TPU:3 before, /device:TPU:13 now
where the time goes in v1:
time: 78.4 us; the launch traced here: 78.1 us
  starting transfers between devices  31.3 us (40%)
  waiting for transfers between devices  21.2 us (27%)
  Pallas kernels  18.2 us (23%)
  local copies, waits for them, and re-layouts  4.82 us (6%)
  other arithmetic  1.67 us (2%)
  between operations  0.88 us (1%)
    ppermute x16, starting transfers between devices, send(): out.append(lax.ppermute(part, AXES, pairs[n]))  29.4 us
    ppermute x16, waiting for transfers between devices, send(): out.append(lax.ppermute(part, AXES, pairs[n]))  20.2 us
    pallas_call x2, Pallas kernels, attend(): pl.pallas_call(functools.partial(attend_kernel, run_blocks, listed, turns...  6.61 us
    unnamed x10, local copies, waits for them, and re-layouts  3.8 us
    pallas_call x2, Pallas kernels, unpack(): pl.pallas_call(functools.partial(unpack_kernel, rounds, width), out_shape...  3.07 us
    pallas_call x1, Pallas kernels, key_grads(): pl.pallas_call(functools.partial(key_grads_kernel, rounds, run_blocks, li...  2.83 us
    pallas_call x1, Pallas kernels, gather(): pl.pallas_call(functools.partial(gather_kernel, rounds), out_shape=[jax.S...  2.11 us
    ppermute x6, starting transfers between devices, swap(): out.append(lax.ppermute(part, 'head', sibling))  1.88 us
  transfers between devices with their start and end apart: 22, of which 8 were waited for; matrix products, arithmetic and copies ran while one was open for 3% of the time, Pallas kernels for 13%

profile of v1, /device:TPU:13, one launch (start us, length us, event | category | flops | bytes accessed | tf_op | source)
XLA Modules:
  0.0 78.1 jit_solution(14492824949815153229)
XLA Ops:
  0.6 0.7 collective-permute-start
  1.4 0.9 %copy-done = bf16[1,256,512]{2,1,0:T(8,128)(2,1)S(1)} copy-done((bf16[1,256,512]{2,1,0:T(8,128)(2,1)S(1)}, bf16[1,256,512]{2,1,0:T(8,128)(2,1)}, u32[]{:S(2)}) %copy-start) | copy-done | bytes 262168
  2.3 0.9 %copy-done.1 = bf16[1,256,512]{2,1,0:T(8,128)(2,1)S(1)} copy-done((bf16[1,256,512]{2,1,0:T(8,128)(2,1)S(1)}, bf16[1,256,512]{2,1,0:T(8,128)(2,1)}, u32[]{:S(2)}) %copy-start.1) | copy-done | bytes 262168
  3.3 0.9 %pack.3 = (bf16[2,256,128]{2,1,0:T(8,128)(2,1)S(1)}, bf16[2,256,128]{2,1,0:T(8,128)(2,1)S(1)}, bf16[2,256,128]{2,1,0:T(8,128)(2,1)S(1)}, bf16[2,256,128]{2,1,0:T(8,128)(2,1)S(1)}) custom-call(s32[1]{0:T(128)} %bitcast.pos_ref, bf16[1,256,512]{2,1,0:T(8,128)(2,1)S(1)} %copy-done, bf16[1,256,512]{2,1,0:T(8,128)(2,1)S(1)} %copy-done.1), custom_call_target="tpu_custom_call" | custom-call | bytes 1048576 | tf_op jit(solution)/shard_map/pack/pallas_call | solution.py:66
  4.2 4.1 %collective-permute-start.9 = (bf16[2,256,128]{2,1,0:T(8,128)(2,1)S(1)}, bf16[2,256,128]{2,1,0:T(8,128)(2,1)S(1)}, u32[]{:S(2)}, u32[]{:S(2)}) collective-permute-start(bf16[2,256,128]{2,1,0:T(8,128)(2,1)S(1)} %get-tuple-element.38), channel_id=1, source_target_pairs={{0,0},{1,16},{2,2},{3,18},{4,4},{5,20},{6,6},{7,22},{8,8},{9,24},{... | collective-permute-start | bytes 393224 | tf_op jit(solution)/shard_map/ppermute | solution.py:443
  8.3 0.0 copy-start.2
  8.3 0.9 %copy-done.2 = bf16[1,256,512]{2,1,0:T(8,128)(2,1)S(1)} copy-done((bf16[1,256,512]{2,1,0:T(8,128)(2,1)S(1)}, bf16[1,256,512]{2,1,0:T(8,128)(2,1)}, u32[]{:S(2)}) %copy-start.2) | copy-done | bytes 262168
  9.3 0.9 %copy-done.3 = bf16[1,256,512]{2,1,0:T(8,128)(2,1)S(1)} copy-done((bf16[1,256,512]{2,1,0:T(8,128)(2,1)S(1)}, bf16[1,256,512]{2,1,0:T(8,128)(2,1)}, u32[]{:S(2)}) %copy-start.3) | copy-done | bytes 262168
  10.2 0.9 %pack.2 = (bf16[2,256,128]{2,1,0:T(8,128)(2,1)S(1)}, bf16[2,256,128]{2,1,0:T(8,128)(2,1)S(1)}, bf16[2,256,128]{2,1,0:T(8,128)(2,1)S(1)}, bf16[2,256,128]{2,1,0:T(8,128)(2,1)S(1)}) custom-call(s32[1]{0:T(128)} %bitcast.pos_ref, bf16[1,256,512]{2,1,0:T(8,128)(2,1)S(1)} %copy-done.2, bf16[1,256,512]{2,1,0:T(8,128)(2,1)S(1)} %copy-done.3), custom_call_target="tpu_custom_call" | custom-call | bytes 1048576 | tf_op jit(solution)/shard_map/pack/pallas_call | solution.py:66
  11.1 2.3 %collective-permute-start.1 = (bf16[2,256,128]{2,1,0:T(8,128)(2,1)S(1)}, bf16[2,256,128]{2,1,0:T(8,128)(2,1)S(1)}, u32[]{:S(2)}, u32[]{:S(2)}) collective-permute-start(bf16[2,256,128]{2,1,0:T(8,128)(2,1)S(1)} %get-tuple-element.32), channel_id=1, source_target_pairs={{0,0},{1,16},{2,2},{3,18},{4,4},{5,20},{6,6},{7,22},{8,8},{9,24},{... | collective-permute-start | bytes 393224 | tf_op jit(solution)/shard_map/ppermute | solution.py:443
  13.5 3.2 %collective-permute-start.2 = (bf16[2,256,128]{2,1,0:T(8,128)(2,1)S(1)}, bf16[2,256,128]{2,1,0:T(8,128)(2,1)S(1)}, u32[]{:S(2)}, u32[]{:S(2)}) collective-permute-start(bf16[2,256,128]{2,1,0:T(8,128)(2,1)S(1)} %get-tuple-element.33), channel_id=1, source_target_pairs={{0,4},{1,20},{2,6},{3,22},{4,0},{5,16},{6,2},{7,18},{8,12},{9,28},... | collective-permute-start | bytes 393224 | tf_op jit(solution)/shard_map/ppermute | solution.py:443
  16.7 0.0 collective-permute-start.3
  16.7 0.1 iota_add_fusion
  16.8 0.1 add.135
  16.8 0.1 add.141
  16.9 0.7 fusion.10
  17.6 0.1 add_clamp_fusion
  17.7 0.1 copy.13.rows_ref
  17.8 0.0 collective-permute-done
  17.9 1.8 %collective-permute-start.4 = (bf16[2,256,128]{2,1,0:T(8,128)(2,1)S(1)}, bf16[2,256,128]{2,1,0:T(8,128)(2,1)S(1)}, u32[]{:S(2)}, u32[]{:S(2)}) collective-permute-start(bf16[2,256,128]{2,1,0:T(8,128)(2,1)S(1)} %get-tuple-element.35), channel_id=1, source_target_pairs={{0,12},{1,28},{2,14},{3,30},{4,8},{5,24},{6,10},{7,26},{8,4},{9,20... | collective-permute-start | bytes 393224 | tf_op jit(solution)/shard_map/ppermute | solution.py:443
  19.6 0.0 collective-permute-done.1.rest_0_
  19.6 0.0 collective-permute-start.5
  19.6 1.6 %collective-permute-done.2.rest_1_ = bf16[2,256,128]{2,1,0:T(8,128)(2,1)S(1)} collective-permute-done((bf16[2,256,128]{2,1,0:T(8,128)(2,1)S(1)}, bf16[2,256,128]{2,1,0:T(8,128)(2,1)S(1)}, u32[]{:S(2)}, u32[]{:S(2)}) %collective-permute-start.2) | collective-permute-done | bytes 131104 | tf_op jit(solution)/shard_map/ppermute | solution.py:443
  21.3 0.0 collective-permute-start.6
  21.3 4.5 %collective-permute-done.3.rest_2_ = bf16[2,256,128]{2,1,0:T(8,128)(2,1)S(1)} collective-permute-done((bf16[2,256,128]{2,1,0:T(8,128)(2,1)S(1)}, bf16[2,256,128]{2,1,0:T(8,128)(2,1)S(1)}, u32[]{:S(2)}, u32[]{:S(2)}) %collective-permute-start.3) | collective-permute-done | bytes 131104 | tf_op jit(solution)/shard_map/ppermute | solution.py:443
  25.7 0.0 collective-permute-start.7
  25.8 0.7 broadcast_select_fusion
  26.4 0.1 copy.14
  26.5 0.6 gather_fusion
  27.1 0.1 pad_add_fusion
  27.2 0.1 concatenate.6
  27.3 0.8 %collective-permute-done.4.rest_3_ = bf16[2,256,128]{2,1,0:T(8,128)(2,1)S(1)} collective-permute-done((bf16[2,256,128]{2,1,0:T(8,128)(2,1)S(1)}, bf16[2,256,128]{2,1,0:T(8,128)(2,1)S(1)}, u32[]{:S(2)}, u32[]{:S(2)}) %collective-permute-start.4) | collective-permute-done | bytes 131104 | tf_op jit(solution)/shard_map/ppermute | solution.py:443
  28.1 0.0 collective-permute-start.10
  28.1 0.0 collective-permute-done.5.rest_4_
  28.1 0.5 collective-permute-start.13
  28.6 0.0 collective-permute-done.6.rest_5_
  28.6 1.7 %collective-permute-start.14 = (bf16[2,256,128]{2,1,0:T(8,128)(2,1)S(1)}, bf16[2,256,128]{2,1,0:T(8,128)(2,1)S(1)}, u32[]{:S(2)}, u32[]{:S(2)}) collective-permute-start(bf16[2,256,128]{2,1,0:T(8,128)(2,1)S(1)} %get-tuple-element.43), channel_id=1, source_target_pairs={{0,12},{1,28},{2,14},{3,30},{4,8},{5,24},{6,10},{7,26},{8,4},{9,20... | collective-permute-start | bytes 393224 | tf_op jit(solution)/shard_map/ppermute | solution.py:443
  30.3 0.0 collective-permute-done.7.rest_6_
  30.3 1.1 %collective-permute-start.8 = (bf16[2,256,128]{2,1,0:T(8,128)(2,1)S(1)}, bf16[2,256,128]{2,1,0:T(8,128)(2,1)S(1)}, u32[]{:S(2)}, u32[]{:S(2)}) collective-permute-start(bf16[2,256,128]{2,1,0:T(8,128)(2,1)S(1)} %collective-permute-done.4.rest_3_), channel_id=1, source_target_pairs={{0,1},{1,0},{2,3},{3,2},{4,5},{5,4},{6,7},{7,6},{8,9},{9,8},{10,11... | collective-permute-start | bytes 393224 | tf_op jit(solution)/shard_map/ppermute | solution.py:449
  31.4 1.0 %collective-permute-done.8.rest_7_ = bf16[2,256,128]{2,1,0:T(8,128)(2,1)S(1)} collective-permute-done((bf16[2,256,128]{2,1,0:T(8,128)(2,1)S(1)}, bf16[2,256,128]{2,1,0:T(8,128)(2,1)S(1)}, u32[]{:S(2)}, u32[]{:S(2)}) %collective-permute-start.8) | collective-permute-done | bytes 131104 | tf_op jit(solution)/shard_map/ppermute | solution.py:449
  32.3 2.1 %gather.7 = (bf16[2,2048,128]{2,1,0:T(8,128)(2,1)S(1)}, bf16[2,128,128]{2,1,0:T(8,128)(2,1)S(1)}) custom-call(s32[128,1]{1,0:T(8,128)S(1)} %copy.13.rows_ref, bf16[2,256,128]{2,1,0:T(8,128)(2,1)S(1)} %collective-permute-done.1.rest_0_, bf16[2,256,128]{2,1,0:T(8,128)(2,1)S(1)} %collective-permute-done.2.rest_1_, ...), custom_call_target="tpu_custom_call" | custom-call | flops 134217728 | bytes 2097152 | tf_op jit(solution)/shard_map/gather/pallas_call | solution.py:172
  34.5 0.0 collective-permute-done.13.rest_0_.rest_2_
  34.5 4.8 %collective-permute-done.14.rest_1_.rest_3_ = bf16[2,256,128]{2,1,0:T(8,128)(2,1)S(1)} collective-permute-done((bf16[2,256,128]{2,1,0:T(8,128)(2,1)S(1)}, bf16[2,256,128]{2,1,0:T(8,128)(2,1)S(1)}, u32[]{:S(2)}, u32[]{:S(2)}) %collective-permute-start.14) | collective-permute-done | bytes 131104 | tf_op jit(solution)/shard_map/ppermute | solution.py:443
  39.2 3.3 %attend.3 = (bf16[2,256,128]{2,1,0:T(8,128)(2,1)S(1)}, bf16[2,256,128]{2,1,0:T(8,128)(2,1)S(1)}, bf16[2,256,512]{2,1,0:T(8,128)(2,1)S(1)}, bf16[2,256,512]{2,1,0:T(8,128)(2,1)S(1)}) custom-call(s32[96]{0:T(128)S(1)} %fusion.8.rows_ref, s32[16]{0:T(128)S(1)} %fusion.4.edge_ref, bf16[2,2048,128]{2,1,0:T(8,128)(2,1)S(1)} %get-tuple-element.36.all_ref, ...), custom_call_target="tpu_custom_call" | custom-call | flops 268435456 | bytes 2097152 | tf_op jit(solution)/shard_map/attend/pallas_call | solution.py:275
  42.6 0.0 collective-permute-done.10.rest_1_
  42.6 3.3 %attend.2 = (bf16[2,256,128]{2,1,0:T(8,128)(2,1)S(1)}, bf16[2,256,128]{2,1,0:T(8,128)(2,1)S(1)}, bf16[2,256,512]{2,1,0:T(8,128)(2,1)S(1)}, bf16[2,256,512]{2,1,0:T(8,128)(2,1)S(1)}) custom-call(s32[96]{0:T(128)S(1)} %fusion.8.rows_ref, s32[16]{0:T(128)S(1)} %fusion.4.edge_ref, bf16[2,2048,128]{2,1,0:T(8,128)(2,1)S(1)} %get-tuple-element.36.all_ref, ...), custom_call_target="tpu_custom_call" | custom-call | flops 268435456 | bytes 2097152 | tf_op jit(solution)/shard_map/attend/pallas_call | solution.py:275
  45.9 0.0 copy-start.4
  45.9 2.8 %key_grads.1 = (f32[2,2176,128]{2,1,0:T(8,128)S(1)}, f32[2,1152,128]{2,1,0:T(8,128)S(1)}) custom-call(s32[96]{0:T(128)S(1)} %fusion.8.rows_ref, bf16[2,256,128]{2,1,0:T(8,128)(2,1)S(1)} %collective-permute-done.9.rest_0_, bf16[2,256,128]{2,1,0:T(8,128)(2,1)S(1)} %collective-permute-done.10.rest_1_, ...), custom_call_target="tpu_custom_call" | custom-call | flops 268435456 | bytes 4194304 | tf_op jit(solution)/shard_map/key_grads/pallas_call | solution.py:347
  48.7 0.1 collective-permute-start.17
  48.8 0.1 collective-permute-start.15
  48.9 1.5 %collective-permute-start.16 = (bf16[2,256,128]{2,1,0:T(8,128)(2,1)S(1)}, bf16[2,256,128]{2,1,0:T(8,128)(2,1)S(1)}, u32[]{:S(2)}, u32[]{:S(2)}) collective-permute-start(bf16[2,256,128]{2,1,0:T(8,128)(2,1)S(1)} %get-tuple-element.45), channel_id=1, source_target_pairs={{0,12},{1,28},{2,14},{3,30},{4,8},{5,24},{6,10},{7,26},{8,4},{9,20... | collective-permute-start | bytes 393224 | tf_op jit(solution)/shard_map/ppermute | solution.py:443
  50.4 6.3 %collective-permute-start.11 = (bf16[2,256,128]{2,1,0:T(8,128)(2,1)S(1)}, bf16[2,256,128]{2,1,0:T(8,128)(2,1)S(1)}, u32[]{:S(2)}, u32[]{:S(2)}) collective-permute-start(bf16[2,256,128]{2,1,0:T(8,128)(2,1)S(1)} %get-tuple-element.40), channel_id=1, source_target_pairs={{0,0},{1,16},{2,2},{3,18},{4,4},{5,20},{6,6},{7,22},{8,8},{9,24},{... | collective-permute-start | bytes 393224 | tf_op jit(solution)/shard_map/ppermute | solution.py:443
  56.7 0.6 collective-permute-start.12
  57.3 1.8 %total.1 = (bf16[2,256,128]{2,1,0:T(8,128)(2,1)S(1)}, bf16[2,256,128]{2,1,0:T(8,128)(2,1)S(1)}, bf16[2,256,128]{2,1,0:T(8,128)(2,1)S(1)}, bf16[2,256,128]{2,1,0:T(8,128)(2,1)S(1)}) custom-call(s32[1,128]{1,0:T(1,128)S(1)} %fusion.9.rows_ref, f32[2,2176,128]{2,1,0:T(8,128)S(1)} %get-tuple-element.52.acc_ref, f32[2,1152,128]{2,1,0:T(8,128)S(1)} %collective-permute-done.17.came_ref), custom_call_target="tpu_custom_call" | custom-call | flops 589824 | bytes 2949120 | tf_op jit(solution)/shard_map/total/pallas_call | solution.py:410
  59.1 4.5 %collective-permute-start.18 = (bf16[2,256,128]{2,1,0:T(8,128)(2,1)S(1)}, bf16[2,256,128]{2,1,0:T(8,128)(2,1)S(1)}, u32[]{:S(2)}, u32[]{:S(2)}) collective-permute-start(bf16[2,256,128]{2,1,0:T(8,128)(2,1)S(1)} %get-tuple-element.54), channel_id=1, source_target_pairs={{0,0},{1,16},{2,2},{3,18},{4,4},{5,20},{6,6},{7,22},{8,8},{9,24},{... | collective-permute-start | bytes 393224 | tf_op jit(solution)/shard_map/ppermute | solution.py:443
  63.7 0.5 collective-permute-start.19
  64.2 0.0 collective-permute-done.16.rest_3_
  64.2 0.2 collective-permute-start.20
  64.4 2.1 %collective-permute-start.21 = (bf16[2,256,128]{2,1,0:T(8,128)(2,1)S(1)}, bf16[2,256,128]{2,1,0:T(8,128)(2,1)S(1)}, u32[]{:S(2)}, u32[]{:S(2)}) collective-permute-start(bf16[2,256,128]{2,1,0:T(8,128)(2,1)S(1)} %get-tuple-element.57), channel_id=1, source_target_pairs={{0,12},{1,28},{2,14},{3,30},{4,8},{5,24},{6,10},{7,26},{8,4},{9,20... | collective-permute-start | bytes 393224 | tf_op jit(solution)/shard_map/ppermute | solution.py:443
  66.4 1.5 %unpack.2 = (bf16[1,256,512]{2,1,0:T(8,128)(2,1)}, bf16[1,256,512]{2,1,0:T(8,128)(2,1)}) custom-call(s32[1]{0:T(128)} %bitcast.pos_ref, bf16[2,256,128]{2,1,0:T(8,128)(2,1)S(1)} %collective-permute-done.11.rest_0_, bf16[2,256,128]{2,1,0:T(8,128)(2,1)S(1)} %collective-permute-done.12.rest_1_, bf16[2,256,128]{2,1,0:T(8,128)(2,1)S(1)} %collective-permute-done.15.rest_2_, ...), custom_call_target="tpu_custom_call" | custom-call | bytes 1048576 | tf_op jit(solution)/shard_map/unpack/pallas_call | solution.py:110
  68.0 3.5 %collective-permute-done.19.rest_1_ = bf16[2,256,128]{2,1,0:T(8,128)(2,1)S(1)} collective-permute-done((bf16[2,256,128]{2,1,0:T(8,128)(2,1)S(1)}, bf16[2,256,128]{2,1,0:T(8,128)(2,1)S(1)}, u32[]{:S(2)}, u32[]{:S(2)}) %collective-permute-start.19) | collective-permute-done | bytes 131104 | tf_op jit(solution)/shard_map/ppermute | solution.py:443
  71.5 3.3 %collective-permute-done.20.rest_2_ = bf16[2,256,128]{2,1,0:T(8,128)(2,1)S(1)} collective-permute-done((bf16[2,256,128]{2,1,0:T(8,128)(2,1)S(1)}, bf16[2,256,128]{2,1,0:T(8,128)(2,1)S(1)}, u32[]{:S(2)}, u32[]{:S(2)}) %collective-permute-start.20) | collective-permute-done | bytes 131104 | tf_op jit(solution)/shard_map/ppermute | solution.py:443
  74.8 1.8 %collective-permute-done.21.rest_3_ = bf16[2,256,128]{2,1,0:T(8,128)(2,1)S(1)} collective-permute-done((bf16[2,256,128]{2,1,0:T(8,128)(2,1)S(1)}, bf16[2,256,128]{2,1,0:T(8,128)(2,1)S(1)}, u32[]{:S(2)}, u32[]{:S(2)}) %collective-permute-start.21) | collective-permute-done | bytes 131104 | tf_op jit(solution)/shard_map/ppermute | solution.py:443
  76.5 1.5 %unpack.3 = (bf16[1,256,512]{2,1,0:T(8,128)(2,1)}, bf16[1,256,512]{2,1,0:T(8,128)(2,1)}) custom-call(s32[1]{0:T(128)} %bitcast.pos_ref, bf16[2,256,128]{2,1,0:T(8,128)(2,1)S(1)} %collective-permute-done.18.rest_0_, bf16[2,256,128]{2,1,0:T(8,128)(2,1)S(1)} %collective-permute-done.19.rest_1_, bf16[2,256,128]{2,1,0:T(8,128)(2,1)S(1)} %collective-permute-done.20.rest_2_, ...), custom_call_target="tpu_custom_call" | custom-call | bytes 1048576 | tf_op jit(solution)/shard_map/unpack/pallas_call | solution.py:110
  (17 shorter events, 0.1 us)
Async XLA Ops:
  0.6 17.2 %collective-permute-start = (s32[1,4,32,3]{2,1,3,0:T(4,128)}, s32[1,4,32,3]{2,1,3,0:T(4,128)S(1)}, u32[]{:S(2)}, u32[]{:S(2)}) collective-permute-start(s32[1,4,32,3]{2,1,3,0:T(4,128)} %param.10), channel_id=1, source_target_pairs={{0,1},{1,0},{2,3},{3,2},{4,5},{5,4},{6,7},{7,6},{8,9},{9,8},{10,11... | collective-permute-start | bytes 4616 | tf_op jit(solution)/shard_map/ppermute | solution.py:449
  1.4 0.9 %copy-start = (bf16[1,256,512]{2,1,0:T(8,128)(2,1)S(1)}, bf16[1,256,512]{2,1,0:T(8,128)(2,1)}, u32[]{:S(2)}) copy-start(bf16[1,256,512]{2,1,0:T(8,128)(2,1)} %a_ref.3) | copy-start | bytes 786436
  2.3 0.9 %copy-start.1 = (bf16[1,256,512]{2,1,0:T(8,128)(2,1)S(1)}, bf16[1,256,512]{2,1,0:T(8,128)(2,1)}, u32[]{:S(2)}) copy-start(bf16[1,256,512]{2,1,0:T(8,128)(2,1)} %b_ref.3) | copy-start | bytes 786436
  4.2 38.4 %collective-permute-start.9 = (bf16[2,256,128]{2,1,0:T(8,128)(2,1)S(1)}, bf16[2,256,128]{2,1,0:T(8,128)(2,1)S(1)}, u32[]{:S(2)}, u32[]{:S(2)}) collective-permute-start(bf16[2,256,128]{2,1,0:T(8,128)(2,1)S(1)} %get-tuple-element.38), channel_id=1, source_target_pairs={{0,0},{1,16},{2,2},{3,18},{4,4},{5,20},{6,6},{7,22},{8,8},{9,24},{... | collective-permute-start | bytes 393224 | tf_op jit(solution)/shard_map/ppermute | solution.py:443
  8.3 1.0 %copy-start.2 = (bf16[1,256,512]{2,1,0:T(8,128)(2,1)S(1)}, bf16[1,256,512]{2,1,0:T(8,128)(2,1)}, u32[]{:S(2)}) copy-start(bf16[1,256,512]{2,1,0:T(8,128)(2,1)} %a_ref.2) | copy-start | bytes 786436
  9.3 0.9 %copy-start.3 = (bf16[1,256,512]{2,1,0:T(8,128)(2,1)S(1)}, bf16[1,256,512]{2,1,0:T(8,128)(2,1)}, u32[]{:S(2)}) copy-start(bf16[1,256,512]{2,1,0:T(8,128)(2,1)} %b_ref.2) | copy-start | bytes 786436
  11.1 8.5 %collective-permute-start.1 = (bf16[2,256,128]{2,1,0:T(8,128)(2,1)S(1)}, bf16[2,256,128]{2,1,0:T(8,128)(2,1)S(1)}, u32[]{:S(2)}, u32[]{:S(2)}) collective-permute-start(bf16[2,256,128]{2,1,0:T(8,128)(2,1)S(1)} %get-tuple-element.32), channel_id=1, source_target_pairs={{0,0},{1,16},{2,2},{3,18},{4,4},{5,20},{6,6},{7,22},{8,8},{9,24},{... | collective-permute-start | bytes 393224 | tf_op jit(solution)/shard_map/ppermute | solution.py:443
  13.5 7.8 %collective-permute-start.2 = (bf16[2,256,128]{2,1,0:T(8,128)(2,1)S(1)}, bf16[2,256,128]{2,1,0:T(8,128)(2,1)S(1)}, u32[]{:S(2)}, u32[]{:S(2)}) collective-permute-start(bf16[2,256,128]{2,1,0:T(8,128)(2,1)S(1)} %get-tuple-element.33), channel_id=1, source_target_pairs={{0,4},{1,20},{2,6},{3,22},{4,0},{5,16},{6,2},{7,18},{8,12},{9,28},... | collective-permute-start | bytes 393224 | tf_op jit(solution)/shard_map/ppermute | solution.py:443
  16.7 9.1 %collective-permute-start.3 = (bf16[2,256,128]{2,1,0:T(8,128)(2,1)S(1)}, bf16[2,256,128]{2,1,0:T(8,128)(2,1)S(1)}, u32[]{:S(2)}, u32[]{:S(2)}) collective-permute-start(bf16[2,256,128]{2,1,0:T(8,128)(2,1)S(1)} %get-tuple-element.34), channel_id=1, source_target_pairs={{0,8},{1,24},{2,10},{3,26},{4,12},{5,28},{6,14},{7,30},{8,0},{9,16... | collective-permute-start | bytes 393224 | tf_op jit(solution)/shard_map/ppermute | solution.py:443
  17.9 10.2 %collective-permute-start.4 = (bf16[2,256,128]{2,1,0:T(8,128)(2,1)S(1)}, bf16[2,256,128]{2,1,0:T(8,128)(2,1)S(1)}, u32[]{:S(2)}, u32[]{:S(2)}) collective-permute-start(bf16[2,256,128]{2,1,0:T(8,128)(2,1)S(1)} %get-tuple-element.35), channel_id=1, source_target_pairs={{0,12},{1,28},{2,14},{3,30},{4,8},{5,24},{6,10},{7,26},{8,4},{9,20... | collective-permute-start | bytes 393224 | tf_op jit(solution)/shard_map/ppermute | solution.py:443
  19.6 8.5 %collective-permute-start.5 = (bf16[2,256,128]{2,1,0:T(8,128)(2,1)S(1)}, bf16[2,256,128]{2,1,0:T(8,128)(2,1)S(1)}, u32[]{:S(2)}, u32[]{:S(2)}) collective-permute-start(bf16[2,256,128]{2,1,0:T(8,128)(2,1)S(1)} %collective-permute-done.1.rest_0_), channel_id=1, source_target_pairs={{0,1},{1,0},{2,3},{3,2},{4,5},{5,4},{6,7},{7,6},{8,9},{9,8},{10,11... | collective-permute-start | bytes 393224 | tf_op jit(solution)/shard_map/ppermute | solution.py:449
  21.3 7.3 %collective-permute-start.6 = (bf16[2,256,128]{2,1,0:T(8,128)(2,1)S(1)}, bf16[2,256,128]{2,1,0:T(8,128)(2,1)S(1)}, u32[]{:S(2)}, u32[]{:S(2)}) collective-permute-start(bf16[2,256,128]{2,1,0:T(8,128)(2,1)S(1)} %collective-permute-done.2.rest_1_), channel_id=1, source_target_pairs={{0,1},{1,0},{2,3},{3,2},{4,5},{5,4},{6,7},{7,6},{8,9},{9,8},{10,11... | collective-permute-start | bytes 393224 | tf_op jit(solution)/shard_map/ppermute | solution.py:449
  25.7 4.5 %collective-permute-start.7 = (bf16[2,256,128]{2,1,0:T(8,128)(2,1)S(1)}, bf16[2,256,128]{2,1,0:T(8,128)(2,1)S(1)}, u32[]{:S(2)}, u32[]{:S(2)}) collective-permute-start(bf16[2,256,128]{2,1,0:T(8,128)(2,1)S(1)} %collective-permute-done.3.rest_2_), channel_id=1, source_target_pairs={{0,1},{1,0},{2,3},{3,2},{4,5},{5,4},{6,7},{7,6},{8,9},{9,8},{10,11... | collective-permute-start | bytes 393224 | tf_op jit(solution)/shard_map/ppermute | solution.py:449
  28.1 14.5 %collective-permute-start.10 = (bf16[2,256,128]{2,1,0:T(8,128)(2,1)S(1)}, bf16[2,256,128]{2,1,0:T(8,128)(2,1)S(1)}, u32[]{:S(2)}, u32[]{:S(2)}) collective-permute-start(bf16[2,256,128]{2,1,0:T(8,128)(2,1)S(1)} %get-tuple-element.39), channel_id=1, source_target_pairs={{0,4},{1,20},{2,6},{3,22},{4,0},{5,16},{6,2},{7,18},{8,12},{9,28},... | collective-permute-start | bytes 393224 | tf_op jit(solution)/shard_map/ppermute | solution.py:443
  28.1 6.4 %collective-permute-start.13 = (bf16[2,256,128]{2,1,0:T(8,128)(2,1)S(1)}, bf16[2,256,128]{2,1,0:T(8,128)(2,1)S(1)}, u32[]{:S(2)}, u32[]{:S(2)}) collective-permute-start(bf16[2,256,128]{2,1,0:T(8,128)(2,1)S(1)} %get-tuple-element.42), channel_id=1, source_target_pairs={{0,8},{1,24},{2,10},{3,26},{4,12},{5,28},{6,14},{7,30},{8,0},{9,16... | collective-permute-start | bytes 393224 | tf_op jit(solution)/shard_map/ppermute | solution.py:443
  28.6 10.6 %collective-permute-start.14 = (bf16[2,256,128]{2,1,0:T(8,128)(2,1)S(1)}, bf16[2,256,128]{2,1,0:T(8,128)(2,1)S(1)}, u32[]{:S(2)}, u32[]{:S(2)}) collective-permute-start(bf16[2,256,128]{2,1,0:T(8,128)(2,1)S(1)} %get-tuple-element.43), channel_id=1, source_target_pairs={{0,12},{1,28},{2,14},{3,30},{4,8},{5,24},{6,10},{7,26},{8,4},{9,20... | collective-permute-start | bytes 393224 | tf_op jit(solution)/shard_map/ppermute | solution.py:443
  30.3 2.0 %collective-permute-start.8 = (bf16[2,256,128]{2,1,0:T(8,128)(2,1)S(1)}, bf16[2,256,128]{2,1,0:T(8,128)(2,1)S(1)}, u32[]{:S(2)}, u32[]{:S(2)}) collective-permute-start(bf16[2,256,128]{2,1,0:T(8,128)(2,1)S(1)} %collective-permute-done.4.rest_3_), channel_id=1, source_target_pairs={{0,1},{1,0},{2,3},{3,2},{4,5},{5,4},{6,7},{7,6},{8,9},{9,8},{10,11... | collective-permute-start | bytes 393224 | tf_op jit(solution)/shard_map/ppermute | solution.py:449
  45.9 10.8 %copy-start.4 = (s32[128]{0:T(128)S(1)}, s32[128]{0:T(128)}, u32[]{:S(2)}) copy-start(s32[128]{0:T(128)} %param.11) | copy-start | bytes 1540
  48.7 8.6 %collective-permute-start.17 = (f32[2,1152,128]{2,1,0:T(8,128)S(1)}, f32[2,1152,128]{2,1,0:T(8,128)S(1)}, u32[]{:S(2)}, u32[]{:S(2)}) collective-permute-start(f32[2,1152,128]{2,1,0:T(8,128)S(1)} %get-tuple-element.53), channel_id=1, source_target_pairs={{0,1},{1,0},{2,3},{3,2},{4,5},{5,4},{6,7},{7,6},{8,9},{9,8},{10,11... | collective-permute-start | bytes 3538952 | tf_op jit(solution)/shard_map/ppermute | solution.py:449
  48.8 14.9 %collective-permute-start.15 = (bf16[2,256,128]{2,1,0:T(8,128)(2,1)S(1)}, bf16[2,256,128]{2,1,0:T(8,128)(2,1)S(1)}, u32[]{:S(2)}, u32[]{:S(2)}) collective-permute-start(bf16[2,256,128]{2,1,0:T(8,128)(2,1)S(1)} %get-tuple-element.44), channel_id=1, source_target_pairs={{0,8},{1,24},{2,10},{3,26},{4,12},{5,28},{6,14},{7,30},{8,0},{9,16... | collective-permute-start | bytes 393224 | tf_op jit(solution)/shard_map/ppermute | solution.py:443
  48.9 15.3 %collective-permute-start.16 = (bf16[2,256,128]{2,1,0:T(8,128)(2,1)S(1)}, bf16[2,256,128]{2,1,0:T(8,128)(2,1)S(1)}, u32[]{:S(2)}, u32[]{:S(2)}) collective-permute-start(bf16[2,256,128]{2,1,0:T(8,128)(2,1)S(1)} %get-tuple-element.45), channel_id=1, source_target_pairs={{0,12},{1,28},{2,14},{3,30},{4,8},{5,24},{6,10},{7,26},{8,4},{9,20... | collective-permute-start | bytes 393224 | tf_op jit(solution)/shard_map/ppermute | solution.py:443
  50.4 14.0 %collective-permute-start.11 = (bf16[2,256,128]{2,1,0:T(8,128)(2,1)S(1)}, bf16[2,256,128]{2,1,0:T(8,128)(2,1)S(1)}, u32[]{:S(2)}, u32[]{:S(2)}) collective-permute-start(bf16[2,256,128]{2,1,0:T(8,128)(2,1)S(1)} %get-tuple-element.40), channel_id=1, source_target_pairs={{0,0},{1,16},{2,2},{3,18},{4,4},{5,20},{6,6},{7,22},{8,8},{9,24},{... | collective-permute-start | bytes 393224 | tf_op jit(solution)/shard_map/ppermute | solution.py:443
  56.7 9.7 %collective-permute-start.12 = (bf16[2,256,128]{2,1,0:T(8,128)(2,1)S(1)}, bf16[2,256,128]{2,1,0:T(8,128)(2,1)S(1)}, u32[]{:S(2)}, u32[]{:S(2)}) collective-permute-start(bf16[2,256,128]{2,1,0:T(8,128)(2,1)S(1)} %get-tuple-element.41), channel_id=1, source_target_pairs={{0,4},{1,20},{2,6},{3,22},{4,0},{5,16},{6,2},{7,18},{8,12},{9,28},... | collective-permute-start | bytes 393224 | tf_op jit(solution)/shard_map/ppermute | solution.py:443
  59.1 8.8 %collective-permute-start.18 = (bf16[2,256,128]{2,1,0:T(8,128)(2,1)S(1)}, bf16[2,256,128]{2,1,0:T(8,128)(2,1)S(1)}, u32[]{:S(2)}, u32[]{:S(2)}) collective-permute-start(bf16[2,256,128]{2,1,0:T(8,128)(2,1)S(1)} %get-tuple-element.54), channel_id=1, source_target_pairs={{0,0},{1,16},{2,2},{3,18},{4,4},{5,20},{6,6},{7,22},{8,8},{9,24},{... | collective-permute-start | bytes 393224 | tf_op jit(solution)/shard_map/ppermute | solution.py:443
  63.7 7.8 %collective-permute-start.19 = (bf16[2,256,128]{2,1,0:T(8,128)(2,1)S(1)}, bf16[2,256,128]{2,1,0:T(8,128)(2,1)S(1)}, u32[]{:S(2)}, u32[]{:S(2)}) collective-permute-start(bf16[2,256,128]{2,1,0:T(8,128)(2,1)S(1)} %get-tuple-element.55), channel_id=1, source_target_pairs={{0,4},{1,20},{2,6},{3,22},{4,0},{5,16},{6,2},{7,18},{8,12},{9,28},... | collective-permute-start | bytes 393224 | tf_op jit(solution)/shard_map/ppermute | solution.py:443
  64.2 10.6 %collective-permute-start.20 = (bf16[2,256,128]{2,1,0:T(8,128)(2,1)S(1)}, bf16[2,256,128]{2,1,0:T(8,128)(2,1)S(1)}, u32[]{:S(2)}, u32[]{:S(2)}) collective-permute-start(bf16[2,256,128]{2,1,0:T(8,128)(2,1)S(1)} %get-tuple-element.56), channel_id=1, source_target_pairs={{0,8},{1,24},{2,10},{3,26},{4,12},{5,28},{6,14},{7,30},{8,0},{9,16... | collective-permute-start | bytes 393224 | tf_op jit(solution)/shard_map/ppermute | solution.py:443
  64.4 12.2 %collective-permute-start.21 = (bf16[2,256,128]{2,1,0:T(8,128)(2,1)S(1)}, bf16[2,256,128]{2,1,0:T(8,128)(2,1)S(1)}, u32[]{:S(2)}, u32[]{:S(2)}) collective-permute-start(bf16[2,256,128]{2,1,0:T(8,128)(2,1)S(1)} %get-tuple-element.57), channel_id=1, source_target_pairs={{0,12},{1,28},{2,14},{3,30},{4,8},{5,24},{6,10},{7,26},{8,4},{9,20... | collective-permute-start | bytes 393224 | tf_op jit(solution)/shard_map/ppermute | solution.py:443
